TPU v7x, 512 devices: a whole 4x4x16 slice. The times are simulated.
512 devices in a mesh: dp: 32 (over z, x_hi), tensor: 16 (over x_lo, y, core).
Axes of the slice: x: 4 (x_hi: 2, x_lo: 2; x = x_hi * 2 + x_lo), y: 4, z: 16, core: 2. Of those that a mesh axis runs over, the one named last changes fastest.
Arguments:
- activations: bfloat16 [2, 128, 256, 4096], P(None, 'dp', None, 'tensor'), may hold values from -6 to 6
- out_grads: bfloat16 [2, 128, 256, 4096], P(None, 'dp', None, 'tensor'), may hold values from -6 to 6
- proj_in: bfloat16 [2, 4096, 64], P(None, 'tensor'), may hold values from -0.09375 to 0.09375
- proj_out: bfloat16 [2, 4096, 64], P(None, 'tensor'), may hold values from -0.09375 to 0.09375
- lengths: int32 [128], P('dp'), may hold values from 32 to 256, as said below
- test_feats: bfloat16 [2, 8192, 4096], P(None, 'dp'), may hold values from -0.0059814453 to 0.0059814453
- test_slot: int32 [8192], P('dp'), may hold values from 0 to 255, as said below
Outputs:
- scores: float32 [128, 1024], P('dp')
Inputs may be any that keep to these rules, and one draw needn't show every extreme that they name: Positions from lengths[e] on are padding; some example has exactly 256 real tokens and some exactly 32. `test_slot`: within each aligned block of 256 test items a permutation of 0 to 255.
All inputs are finite; a program needn't handle non-finite values.
Results may differ from a plain program's by a relative error of at most 0.005.
Values may be sent and summed in bfloat16 or wider, within the bound.
No kernel may reach another device: no remote copies, remote signals or barrier semaphores. Data moves between devices by JAX's collectives and lax.ppermute only.
A program may use at most 128 MiB of HBM per device.

v0:
```python
import jax
import jax.numpy as jnp
from jax import lax
from jax.sharding import PartitionSpec as P

STEPS = 4


def from_behind(value, axis, steps):
    count = lax.axis_size(axis)
    pairs = [(source, (source + steps) % count) for source in range(count)]
    return lax.ppermute(value, axis, pairs)


def score_tile(feat_rows, test_block):
    return jnp.einsum("lef,ltf->et", feat_rows, test_block, preferred_element_type=jnp.float32)


def shards(activations, out_grads, proj_in, proj_out, lengths, test_feats, test_slot):
    low_rank = proj_in.shape[2]
    part_act = jnp.einsum(
        "lesd,ldr->lesr", activations, proj_in, preferred_element_type=jnp.float32
    )
    part_grad = jnp.einsum(
        "lesd,ldr->lesr", out_grads, proj_out, preferred_element_type=jnp.float32
    )
    partial_proj = jnp.concatenate([part_act, part_grad], axis=3)
    summed = lax.psum(partial_proj, "tensor")
    layer_count, example_count, token_count = (summed.shape[0], summed.shape[1], summed.shape[2])
    rounded = summed.astype(jnp.bfloat16)
    positions = jnp.arange(token_count, dtype=jnp.int32)
    kept_mask = (positions[None, :] < lengths[:, None]).astype(jnp.bfloat16)
    grad_side = rounded[..., low_rank:] * kept_mask[None, :, :, None]
    outer_sums = jnp.einsum(
        "lesa,lesb->leab", grad_side, rounded[..., :low_rank], preferred_element_type=jnp.float32
    )
    outer_sums = outer_sums.reshape(layer_count, example_count, low_rank * low_rank)
    features = outer_sums.astype(jnp.bfloat16)
    ordered = jnp.zeros_like(test_feats).at[:, test_slot, :].set(test_feats)
    score_tiles = [score_tile(features, ordered)]
    test_block = ordered
    for distance in range(1, STEPS):
        test_block = from_behind(test_block, "dp", 1)
        score_tiles.append(score_tile(features, test_block))
    return jnp.concatenate(score_tiles, axis=1)


def solution(mesh):
    return jax.shard_map(
        shards,
        mesh=mesh,
        in_specs=(
            P(None, "dp", None, "tensor"),
            P(None, "dp", None, "tensor"),
            P(None, "tensor", None),
            P(None, "tensor", None),
            P("dp"),
            P(None, "dp", None),
            P("dp"),
        ),
        out_specs=P("dp", None),
        check_vma=False,
    )
```

profile of v0, /device:TPU:1, one launch (start us, length us, event | category | flops | bytes accessed | tf_op | source)
XLA Modules:
  0.0 421.6 jit_solution(16732121050060991704)
XLA Ops:
  0.0 0.0 copy-start
  0.0 0.8 compare_select_fusion
  0.8 8.5 %copy.8 = bf16[256,2,4096]{2,1,0:T(2,128)(2,1)} copy(bf16[256,2,4096]{2,0,1:T(8,128)(2,1)} %bitcast.31) | data formatting | bytes 8388608 | tf_op args[5]
  9.3 6.2 %broadcast_in_dim.4 = bf16[2,256,4096]{2,0,1:T(2,128)(2,1)} broadcast(bf16[]{:T(256)} %constant.0.clone.1), dimensions={} | broadcast | bytes 4194306 | tf_op jit(solution)/shard_map/broadcast_in_dim | solution.py:39
  15.5 34.5 %scatter_fusion = bf16[2,256,4096]{2,0,1:T(2,128)(2,1)} fusion(bf16[2,256,4096]{2,0,1:T(2,128)(2,1)} %broadcast_in_dim.4, s32[256]{0:T(256)S(1)} %compare_select_fusion, bf16[256,2,4096]{2,1,0:T(2,128)(2,1)} %copy.8), kind=kCustom, calls=%fused_computation | custom fusion | bytes 12583936 | tf_op jit(solution)/shard_map/scatter | solution.py:39
  49.9 0.0 copy-start.4
  49.9 0.0 copy-start.3
  49.9 0.0 copy-start.5
  49.9 5.2 %copy.9 = bf16[2,256,4096]{2,1,0:T(8,128)(2,1)S(1)} copy(bf16[2,256,4096]{2,0,1:T(2,128)(2,1)} %scatter_fusion) | data formatting | bytes 8388608 | tf_op jit(solution)/shard_map/scatter | solution.py:39
  55.1 0.0 copy-start.6
  55.2 5.5 %collective-permute-start = (bf16[2,256,4096]{2,1,0:T(8,128)(2,1)S(1)}, bf16[2,256,4096]{2,1,0:T(8,128)(2,1)S(1)}, u32[]{:S(2)}, u32[]{:S(2)}) collective-permute-start(bf16[2,256,4096]{2,1,0:T(8,128)(2,1)S(1)} %copy.9), channel_id=1, source_target_pairs={{0,16},{16,32},{32,48},{48,64},{64,80},{80,96},{96,112},{112,128},... | collective-permute-start | bytes 12582920 | tf_op jit(solution)/shard_map/ppermute | solution.py:12
  60.7 99.2 %collective-permute-done = bf16[2,256,4096]{2,1,0:T(8,128)(2,1)S(1)} collective-permute-done((bf16[2,256,4096]{2,1,0:T(8,128)(2,1)S(1)}, bf16[2,256,4096]{2,1,0:T(8,128)(2,1)S(1)}, u32[]{:S(2)}, u32[]{:S(2)}) %collective-permute-start) | collective-permute-done | bytes 4194336 | tf_op jit(solution)/shard_map/ppermute | solution.py:12
  159.9 0.0 copy-start.1
  159.9 2.0 copy-done.1
  161.8 1.9 collective-permute-start.1
  163.7 94.6 %collective-permute-done.1 = bf16[2,256,4096]{2,1,0:T(8,128)(2,1)} collective-permute-done((bf16[2,256,4096]{2,1,0:T(8,128)(2,1)S(1)}, bf16[2,256,4096]{2,1,0:T(8,128)(2,1)}, u32[]{:S(2)}, u32[]{:S(2)}) %collective-permute-start.1) | collective-permute-done | bytes 4194336 | tf_op jit(solution)/shard_map/ppermute | solution.py:12
  258.3 1.9 collective-permute-start.2
  260.2 0.0 copy-done
  260.2 0.0 copy-done.4
  260.2 0.4 fusion.4
  260.7 0.0 copy-done.3
  260.7 0.0 copy-done.5
  260.7 0.4 fusion.2
  261.1 0.1 pad_maximum_fusion
  261.2 0.0 copy-done.6
  261.2 0.1 fusion.6
  261.3 146.6 %all-reduce.1 = bf16[2,4,256,128]{2,3,1,0:T(8,128)(2,1)S(1)} all-reduce(f32[2,4,256,128]{2,3,1,0:T(8,128)S(1)} %pad_maximum_fusion), channel_id=1, replica_groups=mesh['dp'=32,'tensor'=16] {'tensor'}, use_global_device_ids=true, to_apply=%region_0.0 | all-reduce | flops 262144 | bytes 1572864 | tf_op jit(solution)/shard_map/psum | solution.py:28
  407.9 0.2 convolution_convert_fusion
  408.1 0.1 convert_element_type.19
  408.3 0.0 copy-start.2
  408.3 4.7 %convolution_bitcast_fusion.3 = f32[4,256]{1,0:T(4,128)S(1)} fusion(bf16[2,4,4096]{2,1,0:T(4,128)(2,1)S(1)} %convert_element_type.19, bf16[2,256,4096]{2,0,1:T(2,128)(2,1)} %scatter_fusion), kind=kOutput, calls=%fused_computation.5 | convolution fusion | flops 16777216 | bytes 4263936 | tf_op jit(solution)/shard_map/lef,ltf->et/dot_general | solution.py:16
  413.0 0.0 copy-done.2
  413.0 1.2 convolution_bitcast_fusion.2
  414.2 3.4 convolution_bitcast_fusion.1
  417.6 0.0 collective-permute-done.2
  417.6 3.4 convolution_bitcast_fusion
  421.0 0.6 pad_maximum_fusion.1
Async XLA Ops:
  0.0 260.2 %copy-start = (bf16[2,4,256,256]{3,2,1,0:T(8,128)(2,1)S(1)}, bf16[2,4,256,256]{3,2,1,0:T(8,128)(2,1)}, u32[]{:S(2)}) copy-start(bf16[2,4,256,256]{3,2,1,0:T(8,128)(2,1)} %param.7) | copy-start | bytes 3145732
  49.9 210.3 %copy-start.4 = (bf16[2,256,64]{1,2,0:T(8,128)(2,1)S(1)}, bf16[2,256,64]{1,2,0:T(8,128)(2,1)}, u32[]{:S(2)}) copy-start(bf16[2,256,64]{1,2,0:T(8,128)(2,1)} %param.9) | copy-start | bytes 196612
  49.9 210.7 %copy-start.3 = (bf16[2,4,256,256]{3,2,1,0:T(8,128)(2,1)S(1)}, bf16[2,4,256,256]{3,2,1,0:T(8,128)(2,1)}, u32[]{:S(2)}) copy-start(bf16[2,4,256,256]{3,2,1,0:T(8,128)(2,1)} %param.8) | copy-start | bytes 3145732
  49.9 210.7 %copy-start.5 = (bf16[2,256,64]{1,2,0:T(8,128)(2,1)S(1)}, bf16[2,256,64]{1,2,0:T(8,128)(2,1)}, u32[]{:S(2)}) copy-start(bf16[2,256,64]{1,2,0:T(8,128)(2,1)} %param.10) | copy-start | bytes 196612
  55.1 206.1 %copy-start.6 = (s32[4]{0:T(128)S(1)}, s32[4]{0:T(128)}, u32[]{:S(2)}) copy-start(s32[4]{0:T(128)} %param.11) | copy-start | bytes 52
  55.2 104.7 %collective-permute-start = (bf16[2,256,4096]{2,1,0:T(8,128)(2,1)S(1)}, bf16[2,256,4096]{2,1,0:T(8,128)(2,1)S(1)}, u32[]{:S(2)}, u32[]{:S(2)}) collective-permute-start(bf16[2,256,4096]{2,1,0:T(8,128)(2,1)S(1)} %copy.9), channel_id=1, source_target_pairs={{0,16},{16,32},{32,48},{48,64},{64,80},{80,96},{96,112},{112,128},... | collective-permute-start | bytes 12582920 | tf_op jit(solution)/shard_map/ppermute | solution.py:12
  159.9 2.0 copy-start.1
  161.8 96.5 %collective-permute-start.1 = (bf16[2,256,4096]{2,1,0:T(8,128)(2,1)S(1)}, bf16[2,256,4096]{2,1,0:T(8,128)(2,1)}, u32[]{:S(2)}, u32[]{:S(2)}) collective-permute-start(bf16[2,256,4096]{2,1,0:T(8,128)(2,1)S(1)} %collective-permute-done), channel_id=1, source_target_pairs={{0,16},{16,32},{32,48},{48,64},{64,80},{80,96},{96,112},{112,128},... | collective-permute-start | bytes 12582920 | tf_op jit(solution)/shard_map/ppermute | solution.py:12
  258.3 159.3 %collective-permute-start.2 = (bf16[2,256,4096]{2,1,0:T(8,128)(2,1)}, bf16[2,256,4096]{2,1,0:T(8,128)(2,1)}, u32[]{:S(2)}, u32[]{:S(2)}) collective-permute-start(bf16[2,256,4096]{2,1,0:T(8,128)(2,1)} %collective-permute-done.1), channel_id=1, source_target_pairs={{0,16},{16,32},{32,48},{48,64},{64,80},{80,96},{96,112},{112,128},... | collective-permute-start | bytes 12582920 | tf_op jit(solution)/shard_map/ppermute | solution.py:12
  408.3 4.7 %copy-start.2 = (bf16[2,256,4096]{2,1,0:T(8,128)(2,1)S(1)}, bf16[2,256,4096]{2,1,0:T(8,128)(2,1)}, u32[]{:S(2)}) copy-start(bf16[2,256,4096]{2,1,0:T(8,128)(2,1)} %copy-done.1) | copy-start | bytes 12582916
where the time goes:
time: 427 us; the launch traced here: 422 us
  waiting for transfers between devices  194 us (45%)
  blocking collectives  147 us (34%)
  local copies, waits for them, and re-layouts  56.5 us (13%)
  matrix products  13.8 us (3%)
  starting transfers between devices  9.36 us (2%)
    ppermute x3, waiting for transfers between devices, from_behind(): return lax.ppermute(value, axis, pairs)  194 us
    psum x1, blocking collectives, shards(): summed = lax.psum(partial_proj, 'tensor')  147 us
    scatter x2, local copies, waits for them, and re-layouts, shards(): ordered = jnp.zeros_like(test_feats).at[:, test_slot, :].set(test_feats)  39.6 us
    dot_general x4, matrix products, score_tile(): jnp.einsum('lef,ltf->et', feat_rows, test_block, preferred_element_type=j...  12.7 us
    unnamed x15, local copies, waits for them, and re-layouts  10.5 us
    ppermute x3, starting transfers between devices, from_behind(): return lax.ppermute(value, axis, pairs)  9.36 us
  transfers between devices with their start and end apart: 3, of which 2 were waited for; matrix products, arithmetic and copies ran while one was open for 3% of the time, Pallas kernels for 0%

commit v1 on v0

v1 whole, which is shorter than its diff:
```python
import jax
import jax.numpy as jnp
from jax import lax
from jax.sharding import PartitionSpec as P

STEPS = 4
GROUP = 16
HIGH = lax.Precision.HIGHEST


def role(k):
    y0, core = (k >> 1) & 1, k & 1
    tile = y0 + core * (3 - 2 * y0)
    return tile, (k >> 2) & 1


def block_pairs(dp_size):
    pairs = []
    for shard in range(dp_size):
        for k in range(GROUP):
            tile, _ = role(k)
            source = k ^ (8 * (tile & 1))
            pairs.append((((shard - tile) % dp_size) * GROUP + source, shard * GROUP + k))
    return pairs


def split_dot(rows, block):
    high = rows.astype(jnp.bfloat16)
    low = (rows - high.astype(jnp.float32)).astype(jnp.bfloat16)
    both = jnp.concatenate([high, low], axis=0)
    out = jnp.einsum("ef,tf->et", both, block, preferred_element_type=jnp.float32)
    return out[: rows.shape[0]] + out[rows.shape[0] :]


def shards(activations, out_grads, proj_in, proj_out, lengths, test_feats, test_slot):
    layers, examples, tokens, _ = activations.shape
    rank = proj_in.shape[2]
    block, feats = test_feats.shape[1], test_feats.shape[2]
    half_feats, half_tokens = feats // 2, tokens // 2
    k = lax.axis_index("tensor")

    tile, half = role(k)
    layer = (k >> 3) ^ (tile & 1)
    piece = lax.dynamic_slice(test_feats, (layer, 0, half * half_feats), (1, block, half_feats))[0]
    place = (jnp.arange(block, dtype=jnp.int32)[:, None] == test_slot[None, :]).astype(jnp.bfloat16)
    ordered = jnp.dot(place, piece, preferred_element_type=jnp.float32).astype(jnp.bfloat16)
    test_block = lax.ppermute(ordered, ("dp", "tensor"), block_pairs(lax.axis_size("dp")))

    part_act = jnp.einsum("lesd,ldr->lesr", activations, proj_in, preferred_element_type=jnp.float32)
    part_grad = jnp.einsum("lesd,ldr->lesr", out_grads, proj_out, preferred_element_type=jnp.float32)
    part = jnp.concatenate([part_act, part_grad], axis=3).astype(jnp.bfloat16)
    part = part.reshape(GROUP, half_tokens, 2 * rank)
    part = lax.all_to_all(part, "tensor", 0, 0)
    proj = jnp.sum(part.astype(jnp.float32), axis=0)
    position = (k & 1) * half_tokens + jnp.arange(half_tokens, dtype=jnp.int32)
    kept = position < lengths[(k >> 1) & 3]
    grad = jnp.where(kept[:, None], proj[:, rank:], 0.0)
    outer = jnp.einsum("sa,sb->ab", grad, proj[:, :rank], precision=HIGH)
    outer = outer.reshape(2, 1, rank // 4, 2 * rank)
    outer = jnp.broadcast_to(outer, (2, 4, rank // 4, 2 * rank)).reshape(8, rank // 4, 2 * rank)
    groups = [list(range(8)), list(range(8, 16))]
    outer = lax.all_to_all(outer, "tensor", 0, 0, axis_index_groups=groups)
    features = outer.reshape(examples, 2, half_feats).sum(axis=1)

    scores = split_dot(features, test_block)
    scores = lax.all_to_all(jnp.broadcast_to(scores[None], (GROUP, examples, block)), "tensor", 0, 0)
    scores = scores.reshape(2, 2, 4, examples, block).sum(axis=(0, 1))
    return jnp.concatenate([scores[0], scores[2], scores[3], scores[1]], axis=1)


def solution(mesh):
    return jax.shard_map(
        shards,
        mesh=mesh,
        in_specs=(
            P(None, "dp", None, "tensor"),
            P(None, "dp", None, "tensor"),
            P(None, "tensor", None),
            P(None, "tensor", None),
            P("dp"),
            P(None, "dp", None),
            P("dp"),
        ),
        out_specs=P("dp", None),
        check_vma=False,
    )
```

time: 427 us -> 64.4 us (0.15); the launches traced: 422 us -> 64 us
  waiting for transfers between devices: 194 us -> 14.2 us
  blocking collectives: 147 us -> 25.4 us
  local copies, waits for them, and re-layouts: 56.5 us -> 3.54 us
  matrix products: 13.8 us -> 6.39 us
    ppermute x3 -> x1, waiting for transfers between devices: 194 us -> 9.96 us  [shards(): lax.ppermute(ordered, ('dp', 'tensor'), block_pairs(lax.axis_size('dp')))]
    psum x1 -> x0, blocking collectives: 147 us -> none  [shards(): summed = lax.psum(partial_proj, 'tensor')]
    scatter x2 -> x0, local copies, waits for them, and re-layouts: 39.6 us -> none  [shards(): ordered = jnp.zeros_like(test_feats).at[:, test_slot, :].set(test_feats)]
    all_to_all x0 -> x2, blocking collectives: none -> 25.4 us  [the longest x1 17 us: shards(): lax.all_to_all(jnp.broadcast_to(scores[None], (GROUP, examples, block)),...]
    all_to_all x0 -> x1, starting transfers between devices: none -> 10.2 us  [shards(): part = lax.all_to_all(part, 'tensor', 0, 0)]
    dot_general x5 -> x3, matrix products: 12.9 us -> 3.45 us  [the longest x1 1.68 us: shards(): jnp.dot(place, piece, preferred_element_type=jnp.float32)]
    unnamed x15 -> x6, local copies, waits for them, and re-layouts: 10.5 us -> 1.23 us
    ppermute x3 -> x1, starting transfers between devices: 9.36 us -> 2.59 us  [shards(): lax.ppermute(ordered, ('dp', 'tensor'), block_pairs(lax.axis_size('dp')))]
  transfers between devices with their start and end apart: 3 -> 2, of which waited for: 2 -> 2; matrix products, arithmetic and copies ran while one was open for 3% -> 5% of each run, Pallas kernels for 0% -> 0%
where the time goes in v1:
time: 64.4 us; the launch traced here: 64 us
  blocking collectives  25.4 us (39%)
  waiting for transfers between devices  14.2 us (22%)
  starting transfers between devices  12.8 us (20%)
  matrix products  6.39 us (10%)
  local copies, waits for them, and re-layouts  3.54 us (5%)
  other arithmetic  1.51 us (2%)
    all_to_all x1, blocking collectives, shards(): lax.all_to_all(jnp.broadcast_to(scores[None], (GROUP, examples, block)),...  17 us
    all_to_all x1, starting transfers between devices, shards(): part = lax.all_to_all(part, 'tensor', 0, 0)  10.2 us
    ppermute x1, waiting for transfers between devices, shards(): lax.ppermute(ordered, ('dp', 'tensor'), block_pairs(lax.axis_size('dp')))  9.96 us
    all_to_all x1, blocking collectives, shards(): outer = lax.all_to_all(outer, 'tensor', 0, 0, axis_index_groups=groups)  8.47 us
    all_to_all x1, waiting for transfers between devices, shards(): part = lax.all_to_all(part, 'tensor', 0, 0)  4.21 us
    ppermute x1, starting transfers between devices, shards(): lax.ppermute(ordered, ('dp', 'tensor'), block_pairs(lax.axis_size('dp')))  2.59 us
    dot_general x1, matrix products, shards(): jnp.dot(place, piece, preferred_element_type=jnp.float32)  1.68 us
    dot_general x1, matrix products, shards(): jnp.einsum('lesd,ldr->lesr', out_grads, proj_out, preferred_element_type=...  1.66 us
  transfers between devices with their start and end apart: 2, of which 2 were waited for; matrix products, arithmetic and copies ran while one was open for 5% of the time, Pallas kernels for 0%

profile of v1, /device:TPU:1, one launch (start us, length us, event | category | flops | bytes accessed | tf_op | source)
XLA Modules:
  0.0 64.0 jit_solution(10061203165241119075)
XLA Ops:
  0.0 0.0 copy-start
  0.0 0.0 copy-start.1
  0.0 1.2 %copy-done = bf16[2,4,256,256]{3,2,1,0:T(8,128)(2,1)S(1)} copy-done((bf16[2,4,256,256]{3,2,1,0:T(8,128)(2,1)S(1)}, bf16[2,4,256,256]{3,2,1,0:T(8,128)(2,1)}, u32[]{:S(2)}) %copy-start) | copy-done | bytes 1048600
  1.2 1.3 %convolution_convert_fusion.2 = bf16[2,4,256,64]{2,3,1,0:T(8,128)(2,1)S(1)} fusion(bf16[2,4,256,256]{3,2,1,0:T(8,128)(2,1)S(1)} %copy-done, bf16[2,256,64]{1,2,0:T(8,128)(2,1)} %param.9), kind=kOutput, calls=%fused_computation.2 | convolution fusion | flops 67239936 | bytes 1376256 | tf_op jit(solution)/shard_map/lesd,ldr->lesr/dot_general | solution.py:49
  2.5 0.2 copy.18
  2.7 0.0 copy-start.2
  2.7 0.1 concatenate.15
  2.8 1.7 %convolution_convert_fusion.1 = bf16[2,4,256,64]{2,3,1,0:T(8,128)(2,1)S(1)} fusion(bf16[2,4,256,256]{3,2,1,0:T(8,128)(2,1)} %param.8, bf16[2,256,64]{1,2,0:T(8,128)(2,1)} %param.10), kind=kOutput, calls=%fused_computation.1 | convolution fusion | flops 67239936 | bytes 1376256 | tf_op jit(solution)/shard_map/lesd,ldr->lesr/dot_general | solution.py:50
  4.5 0.2 copy.19
  4.7 0.1 concatenate.16
  4.9 1.0 %copy.20 = bf16[16,128,128]{1,2,0:T(8,128)(2,1)} copy(bf16[16,128,128]{1,0,2:T(8,128)(2,1)S(1)} %pad_maximum_fusion) | data formatting | bytes 1048576 | tf_op jit(solution)/shard_map/concatenate | solution.py:51
  5.8 10.2 %all-to-all-start = ((bf16[16,128,128]{1,2,0:T(8,128)(2,1)}), bf16[16,128,128]{1,2,0:T(8,128)(2,1)S(1)}, u32[]{:S(2)}, u32[]{:S(2)}) async-start(bf16[16,128,128]{1,2,0:T(8,128)(2,1)} %copy.20), calls=%async_computation | async-start | bytes 1048576 | tf_op jit(solution)/shard_map/all_to_all | solution.py:53
  16.0 0.0 copy-done.1
  16.0 1.7 %convolution_convert_fusion = bf16[256,2048]{1,0:T(8,128)(2,1)S(1)} fusion(bf16[2,256,4096]{2,1,0:T(8,128)(2,1)} %param.12, s32[]{:T(128)S(6)} %select_n.15, s32[]{:T(128)S(6)} %select_n.16, s32[256]{0:T(256)S(1)} %copy-done.1), kind=kOutput, calls=%fused_computation | convolution fusion | flops 269025280 | bytes 2098184 | tf_op jit(solution)/shard_map/dot_general | solution.py:46
  17.7 2.6 %collective-permute-start = (bf16[256,2048]{1,0:T(8,128)(2,1)S(1)}, bf16[256,2048]{1,0:T(8,128)(2,1)}, u32[]{:S(2)}, u32[]{:S(2)}) collective-permute-start(bf16[256,2048]{1,0:T(8,128)(2,1)S(1)} %convolution_convert_fusion), channel_id=1, source_target_pairs={{0,0},{473,1},{506,2},{483,3},{4,4},{477,5},{510,6},{487,7},{8,8},... | collective-permute-start | bytes 3145736 | tf_op jit(solution)/shard_map/ppermute | solution.py:47
  20.3 0.0 copy-done.2
  20.3 0.6 dynamic_slice.6
  20.9 0.7 %add_compare_fusion = pred[128]{0:T(512)(128)(4,1)S(1)} fusion(s32[]{:T(128)} %bitcast, s32[]{:T(128)S(6)} %mul.12), kind=kLoop, calls=%fused_computation.27 | loop fusion | flops 256 | bytes 136 | tf_op jit(solution)/shard_map/lt | solution.py:56
  21.6 4.2 %all-to-all-done = bf16[16,128,128]{1,2,0:T(8,128)(2,1)S(1)} async-done(((bf16[16,128,128]{1,2,0:T(8,128)(2,1)}), bf16[16,128,128]{1,2,0:T(8,128)(2,1)S(1)}, u32[]{:S(2)}, u32[]{:S(2)}) %all-to-all-start) | async-done | bytes 524320 | tf_op jit(solution)/shard_map/all_to_all | solution.py:53
  25.8 0.1 convert_reduce_fusion
  25.9 0.2 fusion.5
  26.1 0.1 broadcast_in_dim.30
  26.1 8.5 %all_to_all.15 = f32[8,16,128]{2,1,0:T(8,128)S(1)} all-to-all(f32[8,16,128]{2,1,0:T(8,128)S(1)} %bitcast.32), channel_id=1, replica_groups={{0,1,2,3,4,5,6,7},{8,9,10,11,12,13,14,15},{16,17,18,19,20,21,22,23},{24..., dimensions={0} | all-to-all | bytes 131072 | tf_op jit(solution)/shard_map/all_to_all | solution.py:62
  34.7 0.1 reduce_sum.28
  34.8 10.0 %collective-permute-done = bf16[256,2048]{1,0:T(8,128)(2,1)} collective-permute-done((bf16[256,2048]{1,0:T(8,128)(2,1)S(1)}, bf16[256,2048]{1,0:T(8,128)(2,1)}, u32[]{:S(2)}, u32[]{:S(2)}) %collective-permute-start) | collective-permute-done | bytes 1048608 | tf_op jit(solution)/shard_map/ppermute | solution.py:47
  44.7 1.6 %fusion.7 = f32[8,256]{1,0:T(8,128)S(1)} fusion(bf16[256,2048]{1,0:T(8,128)(2,1)} %collective-permute-done, bf16[4,2048]{1,0:T(4,128)(2,1)S(1)} %get-tuple-element.5, bf16[4,2048]{1,0:T(4,128)(2,1)S(1)} %get-tuple-element.6), kind=kOutput, calls=%fused_computation.14 | convolution fusion | flops 8454144 | bytes 1089536 | tf_op jit(solution)/shard_map/ef,tf->et/dot_general | solution.py:31
  46.4 17.0 %all_to_all.16 = f32[16,4,256]{2,1,0:T(4,128)S(1)} all-to-all(f32[16,4,256]{2,1,0:T(4,128)S(1)} %broadcast_in_dim.32), channel_id=1, replica_groups=mesh['dp'=32,'tensor'=16] {'tensor'}, dimensions={0} | all-to-all | bytes 131072 | tf_op jit(solution)/shard_map/all_to_all | solution.py:66
  63.4 0.6 pad_maximum_fusion.1
  (8 shorter events, 0.2 us)
Async XLA Ops:
  0.0 1.2 %copy-start = (bf16[2,4,256,256]{3,2,1,0:T(8,128)(2,1)S(1)}, bf16[2,4,256,256]{3,2,1,0:T(8,128)(2,1)}, u32[]{:S(2)}) copy-start(bf16[2,4,256,256]{3,2,1,0:T(8,128)(2,1)} %param.7) | copy-start | bytes 3145732
  0.0 16.0 %copy-start.1 = (s32[256]{0:T(256)S(1)}, s32[256]{0:T(256)}, u32[]{:S(2)}) copy-start(s32[256]{0:T(256)} %param.13) | copy-start | bytes 3076
  2.7 17.6 %copy-start.2 = (s32[4]{0:T(128)S(1)}, s32[4]{0:T(128)}, u32[]{:S(2)}) copy-start(s32[4]{0:T(128)} %param.11) | copy-start | bytes 52
  5.8 20.0 %all-to-all-start = ((bf16[16,128,128]{1,2,0:T(8,128)(2,1)}), bf16[16,128,128]{1,2,0:T(8,128)(2,1)S(1)}, u32[]{:S(2)}, u32[]{:S(2)}) async-start(bf16[16,128,128]{1,2,0:T(8,128)(2,1)} %copy.20), calls=%async_computation | async-start | bytes 1048576 | tf_op jit(solution)/shard_map/all_to_all | solution.py:53
  17.7 27.0 %collective-permute-start = (bf16[256,2048]{1,0:T(8,128)(2,1)S(1)}, bf16[256,2048]{1,0:T(8,128)(2,1)}, u32[]{:S(2)}, u32[]{:S(2)}) collective-permute-start(bf16[256,2048]{1,0:T(8,128)(2,1)S(1)} %convolution_convert_fusion), channel_id=1, source_target_pairs={{0,0},{473,1},{506,2},{483,3},{4,4},{477,5},{510,6},{487,7},{8,8},... | collective-permute-start | bytes 3145736 | tf_op jit(solution)/shard_map/ppermute | solution.py:47

commit v2 on v1

--- a/solution.py
+++ b/solution.py
@@ -1,9 +1,10 @@
 import jax
 import jax.numpy as jnp
 from jax import lax
+from jax.experimental import pallas as pl
+from jax.experimental.pallas import tpu as pltpu
 from jax.sharding import PartitionSpec as P
 
-STEPS = 4
 GROUP = 16
 HIGH = lax.Precision.HIGHEST
 
@@ -32,8 +33,60 @@
     return out[: rows.shape[0]] + out[rows.shape[0] :]
 
 
+def project_kernel(act_hbm, grad_hbm, in_hbm, out_hbm, part_ref, rows, matrices, sems):
+    layers, examples, tokens, width = act_hbm.shape
+    rank = in_hbm.shape[1]
+    count = layers * examples
+    loads = [
+        pltpu.make_async_copy(in_hbm, matrices.at[0], sems.at[2 * count]),
+        pltpu.make_async_copy(out_hbm, matrices.at[1], sems.at[2 * count + 1]),
+    ]
+    for i in range(count):
+        layer, example = divmod(i, examples)
+        loads.append(pltpu.make_async_copy(act_hbm.at[layer, example], rows.at[0, i], sems.at[i]))
+        loads.append(pltpu.make_async_copy(grad_hbm.at[layer, example], rows.at[1, i], sems.at[count + i]))
+    for load in loads:
+        load.start()
+    loads[0].wait()
+    loads[1].wait()
+    empty = jnp.zeros((rank, width), jnp.bfloat16)
+    for layer in range(layers):
+        left = jnp.concatenate([matrices[0, layer], empty], axis=1)
+        right = jnp.concatenate([empty, matrices[1, layer]], axis=1)
+        matrix = jnp.concatenate([left, right], axis=0)
+        for example in range(examples):
+            i = layer * examples + example
+            loads[2 * i + 2].wait()
+            loads[2 * i + 3].wait()
+            both = jnp.concatenate([rows[0, i], rows[1, i]], axis=1)
+            part = lax.dot_general(
+                both, matrix, (((1,), (1,)), ((), ())), preferred_element_type=jnp.float32
+            ).astype(jnp.bfloat16)
+            part_ref[2 * i] = part[: tokens // 2]
+            part_ref[2 * i + 1] = part[tokens // 2 :]
+
+
+def project(activations, out_grads, proj_in, proj_out):
+    layers, examples, tokens, width = activations.shape
+    rank = proj_in.shape[2]
+    count = layers * examples
+    return pl.pallas_call(
+        project_kernel,
+        out_shape=jax.ShapeDtypeStruct((2 * count, tokens // 2, 2 * rank), jnp.bfloat16),
+        in_specs=[pl.BlockSpec(memory_space=pltpu.HBM)] * 4,
+        out_specs=pl.BlockSpec(memory_space=pltpu.VMEM),
+        scratch_shapes=[
+            pltpu.VMEM((2, count, tokens, width), jnp.bfloat16),
+            pltpu.VMEM((2, layers, rank, width), jnp.bfloat16),
+            pltpu.SemaphoreType.DMA((2 * count + 2,)),
+        ],
+        cost_estimate=pl.CostEstimate(flops=2**29, bytes_accessed=2**21, transcendentals=0),
+        name="project",
+    )(activations, out_grads, jnp.swapaxes(proj_in, 1, 2), jnp.swapaxes(proj_out, 1, 2))
+
+
 def shards(activations, out_grads, proj_in, proj_out, lengths, test_feats, test_slot):
-    layers, examples, tokens, _ = activations.shape
+    _, examples, tokens, _ = activations.shape
     rank = proj_in.shape[2]
     block, feats = test_feats.shape[1], test_feats.shape[2]
     half_feats, half_tokens = feats // 2, tokens // 2
@@ -46,10 +99,7 @@
     ordered = jnp.dot(place, piece, preferred_element_type=jnp.float32).astype(jnp.bfloat16)
     test_block = lax.ppermute(ordered, ("dp", "tensor"), block_pairs(lax.axis_size("dp")))
 
-    part_act = jnp.einsum("lesd,ldr->lesr", activations, proj_in, preferred_element_type=jnp.float32)
-    part_grad = jnp.einsum("lesd,ldr->lesr", out_grads, proj_out, preferred_element_type=jnp.float32)
-    part = jnp.concatenate([part_act, part_grad], axis=3).astype(jnp.bfloat16)
-    part = part.reshape(GROUP, half_tokens, 2 * rank)
+    part = project(activations, out_grads, proj_in, proj_out)
     part = lax.all_to_all(part, "tensor", 0, 0)
     proj = jnp.sum(part.astype(jnp.float32), axis=0)
     position = (k & 1) * half_tokens + jnp.arange(half_tokens, dtype=jnp.int32)

time: 64.4 us -> 61.3 us (0.952)
  Pallas kernels: 0 us -> 4.13 us
  matrix products: 6.39 us -> 2.39 us
  local copies, waits for them, and re-layouts: 3.54 us -> 0.73 us
    pallas_call x0 -> x1, Pallas kernels: none -> 4.13 us  [project(): pl.pallas_call(project_kernel, out_shape=jax.ShapeDtypeStruct((2 * count,...]
    dot_general x2 -> x0, matrix products: 2.94 us -> none  [the longest x1 1.66 us: shards(): jnp.einsum('lesd,ldr->lesr', out_grads, proj_out, preferred_element_type=...]
    unnamed x6 -> x2, local copies, waits for them, and re-layouts: 1.23 us -> 0.01 us
    dot_general x1, matrix products: 1.59 us -> 0.37 us  [split_dot(): jnp.einsum('ef,tf->et', both, block, preferred_element_type=jnp.float32)]
    concatenate x3 -> x0, local copies, waits for them, and re-layouts: 1.16 us -> none  [shards(): part = jnp.concatenate([part_act, part_grad], axis=3).astype(jnp.bfloat16)]
  transfers between devices with their start and end apart: 2 -> 2, of which waited for: 2 -> 2; matrix products, arithmetic and copies ran while one was open for 5% -> 6% of each run, Pallas kernels for 0% -> 0%
where the time goes in v2:
time: 61.3 us; the launch traced here: 61 us
  blocking collectives  25.4 us (41%)
  waiting for transfers between devices  13.9 us (23%)
  starting transfers between devices  12.8 us (21%)
  Pallas kernels  4.13 us (7%)
  matrix products  2.39 us (4%)
  other arithmetic  1.46 us (2%)
  local copies, waits for them, and re-layouts  0.73 us (1%)
    all_to_all x1, blocking collectives, shards(): lax.all_to_all(jnp.broadcast_to(scores[None], (GROUP, examples, block)),...  17 us
    all_to_all x1, starting transfers between devices, shards(): part = lax.all_to_all(part, 'tensor', 0, 0)  10.2 us
    ppermute x1, waiting for transfers between devices, shards(): lax.ppermute(ordered, ('dp', 'tensor'), block_pairs(lax.axis_size('dp')))  9.7 us
    all_to_all x1, blocking collectives, shards(): outer = lax.all_to_all(outer, 'tensor', 0, 0, axis_index_groups=groups)  8.47 us
    all_to_all x1, waiting for transfers between devices, shards(): part = lax.all_to_all(part, 'tensor', 0, 0)  4.2 us
    pallas_call x1, Pallas kernels, project(): pl.pallas_call(project_kernel, out_shape=jax.ShapeDtypeStruct((2 * count,...  4.13 us
    ppermute x1, starting transfers between devices, shards(): lax.ppermute(ordered, ('dp', 'tensor'), block_pairs(lax.axis_size('dp')))  2.59 us
    dot_general x1, matrix products, shards(): jnp.dot(place, piece, preferred_element_type=jnp.float32)  1.69 us
  transfers between devices with their start and end apart: 2, of which 2 were waited for; matrix products, arithmetic and copies ran while one was open for 6% of the time, Pallas kernels for 0%

profile of v2, /device:TPU:1, one launch (start us, length us, event | category | flops | bytes accessed | tf_op | source)
XLA Modules:
  0.0 61.0 jit_solution(15133598051344244959)
XLA Ops:
  0.0 0.0 copy-start
  0.0 4.1 %project.1 = bf16[16,128,128]{2,1,0:T(8,128)(2,1)} custom-call(bf16[2,4,256,256]{3,2,1,0:T(8,128)(2,1)} %act_hbm.1, bf16[2,4,256,256]{3,2,1,0:T(8,128)(2,1)} %grad_hbm.1, bf16[2,64,256]{2,1,0:T(8,128)(2,1)} %bitcast.19, bf16[2,64,256]{2,1,0:T(8,128)(2,1)} %bitcast.20), custom_call_target="tpu_custom_call" | custom-call | flops 536870912 | bytes 2097152 | tf_op jit(solution)/shard_map/project/pallas_call | solution.py:73
  4.1 10.2 %all-to-all-start = ((bf16[16,128,128]{2,1,0:T(8,128)(2,1)}), bf16[16,128,128]{2,1,0:T(8,128)(2,1)S(1)}, u32[]{:S(2)}, u32[]{:S(2)}) async-start(bf16[16,128,128]{2,1,0:T(8,128)(2,1)} %project.1), calls=%async_computation | async-start | bytes 1048576 | tf_op jit(solution)/shard_map/all_to_all | solution.py:103
  14.4 1.7 %convolution_convert_fusion = bf16[256,2048]{1,0:T(8,128)(2,1)S(1)} fusion(bf16[2,256,4096]{2,1,0:T(8,128)(2,1)} %param.12, s32[]{:T(128)S(6)} %select_n.15, s32[]{:T(128)S(6)} %select_n.16, s32[256]{0:T(256)} %param.13), kind=kOutput, calls=%fused_computation | convolution fusion | flops 269025280 | bytes 2098184 | tf_op jit(solution)/shard_map/dot_general | solution.py:99
  16.0 2.6 %collective-permute-start = (bf16[256,2048]{1,0:T(8,128)(2,1)S(1)}, bf16[256,2048]{1,0:T(8,128)(2,1)S(1)}, u32[]{:S(2)}, u32[]{:S(2)}) collective-permute-start(bf16[256,2048]{1,0:T(8,128)(2,1)S(1)} %convolution_convert_fusion), channel_id=1, source_target_pairs={{0,0},{473,1},{506,2},{483,3},{4,4},{477,5},{510,6},{487,7},{8,8},... | collective-permute-start | bytes 3145736 | tf_op jit(solution)/shard_map/ppermute | solution.py:100
  18.6 0.0 copy-done
  18.7 0.6 dynamic_slice.6
  19.2 0.7 %add_compare_fusion = pred[128]{0:T(512)(128)(4,1)S(1)} fusion(s32[]{:T(128)} %bitcast, s32[]{:T(128)S(6)} %mul.12), kind=kLoop, calls=%fused_computation.22 | loop fusion | flops 256 | bytes 136 | tf_op jit(solution)/shard_map/lt | solution.py:106
  19.9 4.2 %all-to-all-done = bf16[16,128,128]{2,1,0:T(8,128)(2,1)S(1)} async-done(((bf16[16,128,128]{2,1,0:T(8,128)(2,1)}), bf16[16,128,128]{2,1,0:T(8,128)(2,1)S(1)}, u32[]{:S(2)}, u32[]{:S(2)}) %all-to-all-start) | async-done | bytes 524320 | tf_op jit(solution)/shard_map/all_to_all | solution.py:103
  24.1 0.1 convert_reduce_fusion
  24.2 0.3 fusion.3
  24.5 0.1 broadcast_in_dim.30
  24.6 8.5 %all_to_all.15 = f32[8,16,128]{2,1,0:T(8,128)S(1)} all-to-all(f32[8,16,128]{2,1,0:T(8,128)S(1)} %bitcast.18), channel_id=1, replica_groups={{0,1,2,3,4,5,6,7},{8,9,10,11,12,13,14,15},{16,17,18,19,20,21,22,23},{24..., dimensions={0} | all-to-all | bytes 131072 | tf_op jit(solution)/shard_map/all_to_all | solution.py:112
  33.1 0.1 reduce_sum.28
  33.2 9.7 %collective-permute-done = bf16[256,2048]{1,0:T(8,128)(2,1)S(1)} collective-permute-done((bf16[256,2048]{1,0:T(8,128)(2,1)S(1)}, bf16[256,2048]{1,0:T(8,128)(2,1)S(1)}, u32[]{:S(2)}, u32[]{:S(2)}) %collective-permute-start) | collective-permute-done | bytes 1048608 | tf_op jit(solution)/shard_map/ppermute | solution.py:100
  42.9 0.4 fusion.5
  43.3 17.0 %all_to_all.16 = f32[16,4,256]{2,1,0:T(4,128)S(1)} all-to-all(f32[16,4,256]{2,1,0:T(4,128)S(1)} %broadcast_in_dim.32), channel_id=1, replica_groups=mesh['dp'=32,'tensor'=16] {'tensor'}, dimensions={0} | all-to-all | bytes 131072 | tf_op jit(solution)/shard_map/all_to_all | solution.py:116
  60.3 0.6 %pad_maximum_fusion = f32[4,1024]{1,0:T(4,128)} fusion(f32[4,256]{1,0:T(4,128)S(1)} %get-tuple-element.8, f32[4,256]{1,0:T(4,128)S(1)} %get-tuple-element.9, f32[4,256]{1,0:T(4,128)S(1)} %get-tuple-element.10, f32[4,256]{1,0:T(4,128)S(1)} %get-tuple-element.7), kind=kLoop, calls=%fused_computation.16 | loop fusion | flops 12288 | bytes 32768 | tf_op jit(solution)/shard_map/concatenate | solution.py:118
  (7 shorter events, 0.1 us)
Async XLA Ops:
  0.0 18.6 %copy-start = (s32[4]{0:T(128)S(1)}, s32[4]{0:T(128)}, u32[]{:S(2)}) copy-start(s32[4]{0:T(128)} %param.11) | copy-start | bytes 52
  4.1 20.0 %all-to-all-start = ((bf16[16,128,128]{2,1,0:T(8,128)(2,1)}), bf16[16,128,128]{2,1,0:T(8,128)(2,1)S(1)}, u32[]{:S(2)}, u32[]{:S(2)}) async-start(bf16[16,128,128]{2,1,0:T(8,128)(2,1)} %project.1), calls=%async_computation | async-start | bytes 1048576 | tf_op jit(solution)/shard_map/all_to_all | solution.py:103
  16.0 26.9 %collective-permute-start = (bf16[256,2048]{1,0:T(8,128)(2,1)S(1)}, bf16[256,2048]{1,0:T(8,128)(2,1)S(1)}, u32[]{:S(2)}, u32[]{:S(2)}) collective-permute-start(bf16[256,2048]{1,0:T(8,128)(2,1)S(1)} %convolution_convert_fusion), channel_id=1, source_target_pairs={{0,0},{473,1},{506,2},{483,3},{4,4},{477,5},{510,6},{487,7},{8,8},... | collective-permute-start | bytes 3145736 | tf_op jit(solution)/shard_map/ppermute | solution.py:100

commit v3 on v2

--- a/solution.py
+++ b/solution.py
@@ -34,7 +34,7 @@
 
 
 def project_kernel(act_hbm, grad_hbm, in_hbm, out_hbm, part_ref, rows, matrices, sems):
-    layers, examples, tokens, width = act_hbm.shape
+    layers, examples, tokens, _ = act_hbm.shape
     rank = in_hbm.shape[1]
     count = layers * examples
     loads = [
@@ -49,21 +49,18 @@
         load.start()
     loads[0].wait()
     loads[1].wait()
-    empty = jnp.zeros((rank, width), jnp.bfloat16)
-    for layer in range(layers):
-        left = jnp.concatenate([matrices[0, layer], empty], axis=1)
-        right = jnp.concatenate([empty, matrices[1, layer]], axis=1)
-        matrix = jnp.concatenate([left, right], axis=0)
-        for example in range(examples):
-            i = layer * examples + example
-            loads[2 * i + 2].wait()
-            loads[2 * i + 3].wait()
-            both = jnp.concatenate([rows[0, i], rows[1, i]], axis=1)
+    for i in range(count):
+        for side in range(2):
+            loads[2 * i + 2 + side].wait()
             part = lax.dot_general(
-                both, matrix, (((1,), (1,)), ((), ())), preferred_element_type=jnp.float32
+                matrices[side, i // examples],
+                rows[side, i],
+                (((1,), (1,)), ((), ())),
+                preferred_element_type=jnp.float32,
             ).astype(jnp.bfloat16)
-            part_ref[2 * i] = part[: tokens // 2]
-            part_ref[2 * i + 1] = part[tokens // 2 :]
+            ranks = pl.ds(side * rank, rank)
+            part_ref[2 * i, ranks] = part[:, : tokens // 2]
+            part_ref[2 * i + 1, ranks] = part[:, tokens // 2 :]
 
 
 def project(activations, out_grads, proj_in, proj_out):
@@ -72,7 +69,7 @@
     count = layers * examples
     return pl.pallas_call(
         project_kernel,
-        out_shape=jax.ShapeDtypeStruct((2 * count, tokens // 2, 2 * rank), jnp.bfloat16),
+        out_shape=jax.ShapeDtypeStruct((2 * count, 2 * rank, tokens // 2), jnp.bfloat16),
         in_specs=[pl.BlockSpec(memory_space=pltpu.HBM)] * 4,
         out_specs=pl.BlockSpec(memory_space=pltpu.VMEM),
         scratch_shapes=[
@@ -104,8 +101,8 @@
     proj = jnp.sum(part.astype(jnp.float32), axis=0)
     position = (k & 1) * half_tokens + jnp.arange(half_tokens, dtype=jnp.int32)
     kept = position < lengths[(k >> 1) & 3]
-    grad = jnp.where(kept[:, None], proj[:, rank:], 0.0)
-    outer = jnp.einsum("sa,sb->ab", grad, proj[:, :rank], precision=HIGH)
+    grad = jnp.where(kept[None, :], proj[rank:], 0.0)
+    outer = jnp.einsum("as,bs->ab", grad, proj[:rank], precision=HIGH)
     outer = outer.reshape(2, 1, rank // 4, 2 * rank)
     outer = jnp.broadcast_to(outer, (2, 4, rank // 4, 2 * rank)).reshape(8, rank // 4, 2 * rank)
     groups = [list(range(8)), list(range(8, 16))]

time: 61.3 us -> 62.2 us (1.015)
  Pallas kernels: 4.13 us -> 5.1 us
    pallas_call x1, Pallas kernels: 4.13 us -> 5.1 us  [project(): pl.pallas_call(project_kernel, out_shape=jax.ShapeDtypeStruct((2 * count,...]
  transfers between devices with their start and end apart: 2 -> 2, of which waited for: 2 -> 2; matrix products, arithmetic and copies ran while one was open for 6% -> 5% of each run, Pallas kernels for 0% -> 0%
where the time goes in v3:
time: 62.2 us; the launch traced here: 61.9 us
  blocking collectives  25.4 us (41%)
  waiting for transfers between devices  14 us (23%)
  starting transfers between devices  12.8 us (21%)
  Pallas kernels  5.1 us (8%)
  matrix products  2.24 us (4%)
  other arithmetic  1.46 us (2%)
  local copies, waits for them, and re-layouts  0.73 us (1%)
    all_to_all x1, blocking collectives, shards(): lax.all_to_all(jnp.broadcast_to(scores[None], (GROUP, examples, block)),...  17 us
    all_to_all x1, starting transfers between devices, shards(): part = lax.all_to_all(part, 'tensor', 0, 0)  10.2 us
    ppermute x1, waiting for transfers between devices, shards(): lax.ppermute(ordered, ('dp', 'tensor'), block_pairs(lax.axis_size('dp')))  9.85 us
    all_to_all x1, blocking collectives, shards(): outer = lax.all_to_all(outer, 'tensor', 0, 0, axis_index_groups=groups)  8.47 us
    pallas_call x1, Pallas kernels, project(): pl.pallas_call(project_kernel, out_shape=jax.ShapeDtypeStruct((2 * count,...  5.1 us
    all_to_all x1, waiting for transfers between devices, shards(): part = lax.all_to_all(part, 'tensor', 0, 0)  4.2 us
    ppermute x1, starting transfers between devices, shards(): lax.ppermute(ordered, ('dp', 'tensor'), block_pairs(lax.axis_size('dp')))  2.59 us
    dot_general x1, matrix products, shards(): jnp.dot(place, piece, preferred_element_type=jnp.float32)  1.69 us
  transfers between devices with their start and end apart: 2, of which 2 were waited for; matrix products, arithmetic and copies ran while one was open for 5% of the time, Pallas kernels for 0%

profile of v3, /device:TPU:1, one launch (start us, length us, event | category | flops | bytes accessed | tf_op | source)
XLA Modules:
  0.0 61.9 jit_solution(5576115773585847814)
XLA Ops:
  0.0 0.0 copy-start
  0.0 5.1 %project.1 = bf16[16,128,128]{2,1,0:T(8,128)(2,1)} custom-call(bf16[2,4,256,256]{3,2,1,0:T(8,128)(2,1)} %act_hbm.1, bf16[2,4,256,256]{3,2,1,0:T(8,128)(2,1)} %grad_hbm.1, bf16[2,64,256]{2,1,0:T(8,128)(2,1)} %bitcast.19, bf16[2,64,256]{2,1,0:T(8,128)(2,1)} %bitcast.20), custom_call_target="tpu_custom_call" | custom-call | flops 536870912 | bytes 2097152 | tf_op jit(solution)/shard_map/project/pallas_call | solution.py:70
  5.1 10.2 %all-to-all-start = ((bf16[16,128,128]{2,1,0:T(8,128)(2,1)}), bf16[16,128,128]{2,1,0:T(8,128)(2,1)S(1)}, u32[]{:S(2)}, u32[]{:S(2)}) async-start(bf16[16,128,128]{2,1,0:T(8,128)(2,1)} %project.1), calls=%async_computation | async-start | bytes 1048576 | tf_op jit(solution)/shard_map/all_to_all | solution.py:100
  15.3 1.7 %convolution_convert_fusion = bf16[256,2048]{1,0:T(8,128)(2,1)S(1)} fusion(bf16[2,256,4096]{2,1,0:T(8,128)(2,1)} %param.12, s32[]{:T(128)S(6)} %select_n.15, s32[]{:T(128)S(6)} %select_n.16, s32[256]{0:T(256)} %param.13), kind=kOutput, calls=%fused_computation | convolution fusion | flops 269025280 | bytes 2098184 | tf_op jit(solution)/shard_map/dot_general | solution.py:96
  17.0 2.6 %collective-permute-start = (bf16[256,2048]{1,0:T(8,128)(2,1)S(1)}, bf16[256,2048]{1,0:T(8,128)(2,1)S(1)}, u32[]{:S(2)}, u32[]{:S(2)}) collective-permute-start(bf16[256,2048]{1,0:T(8,128)(2,1)S(1)} %convolution_convert_fusion), channel_id=1, source_target_pairs={{0,0},{473,1},{506,2},{483,3},{4,4},{477,5},{510,6},{487,7},{8,8},... | collective-permute-start | bytes 3145736 | tf_op jit(solution)/shard_map/ppermute | solution.py:97
  19.6 0.0 copy-done
  19.6 0.6 dynamic_slice.6
  20.2 0.7 %add_compare_fusion = pred[128]{0:T(512)(128)(4,1)S(1)} fusion(s32[]{:T(128)} %bitcast, s32[]{:T(128)S(6)} %mul.12), kind=kLoop, calls=%fused_computation.22 | loop fusion | flops 256 | bytes 136 | tf_op jit(solution)/shard_map/lt | solution.py:103
  20.9 4.2 %all-to-all-done = bf16[16,128,128]{2,1,0:T(8,128)(2,1)S(1)} async-done(((bf16[16,128,128]{2,1,0:T(8,128)(2,1)}), bf16[16,128,128]{2,1,0:T(8,128)(2,1)S(1)}, u32[]{:S(2)}, u32[]{:S(2)}) %all-to-all-start) | async-done | bytes 524320 | tf_op jit(solution)/shard_map/all_to_all | solution.py:100
  25.1 0.1 convert_reduce_fusion
  25.1 0.2 fusion.3
  25.3 0.1 broadcast_in_dim.30
  25.4 8.5 %all_to_all.15 = f32[8,16,128]{2,1,0:T(8,128)S(1)} all-to-all(f32[8,16,128]{2,1,0:T(8,128)S(1)} %bitcast.18), channel_id=1, replica_groups={{0,1,2,3,4,5,6,7},{8,9,10,11,12,13,14,15},{16,17,18,19,20,21,22,23},{24..., dimensions={0} | all-to-all | bytes 131072 | tf_op jit(solution)/shard_map/all_to_all | solution.py:109
  33.9 0.1 reduce_sum.28
  34.0 9.8 %collective-permute-done = bf16[256,2048]{1,0:T(8,128)(2,1)S(1)} collective-permute-done((bf16[256,2048]{1,0:T(8,128)(2,1)S(1)}, bf16[256,2048]{1,0:T(8,128)(2,1)S(1)}, u32[]{:S(2)}, u32[]{:S(2)}) %collective-permute-start) | collective-permute-done | bytes 1048608 | tf_op jit(solution)/shard_map/ppermute | solution.py:97
  43.9 0.4 fusion.5
  44.3 17.0 %all_to_all.16 = f32[16,4,256]{2,1,0:T(4,128)S(1)} all-to-all(f32[16,4,256]{2,1,0:T(4,128)S(1)} %broadcast_in_dim.32), channel_id=1, replica_groups=mesh['dp'=32,'tensor'=16] {'tensor'}, dimensions={0} | all-to-all | bytes 131072 | tf_op jit(solution)/shard_map/all_to_all | solution.py:113
  61.3 0.6 pad_maximum_fusion
  (7 shorter events, 0.1 us)
Async XLA Ops:
  0.0 19.6 %copy-start = (s32[4]{0:T(128)S(1)}, s32[4]{0:T(128)}, u32[]{:S(2)}) copy-start(s32[4]{0:T(128)} %param.11) | copy-start | bytes 52
  5.1 20.0 %all-to-all-start = ((bf16[16,128,128]{2,1,0:T(8,128)(2,1)}), bf16[16,128,128]{2,1,0:T(8,128)(2,1)S(1)}, u32[]{:S(2)}, u32[]{:S(2)}) async-start(bf16[16,128,128]{2,1,0:T(8,128)(2,1)} %project.1), calls=%async_computation | async-start | bytes 1048576 | tf_op jit(solution)/shard_map/all_to_all | solution.py:100
  17.0 26.9 %collective-permute-start = (bf16[256,2048]{1,0:T(8,128)(2,1)S(1)}, bf16[256,2048]{1,0:T(8,128)(2,1)S(1)}, u32[]{:S(2)}, u32[]{:S(2)}) collective-permute-start(bf16[256,2048]{1,0:T(8,128)(2,1)S(1)} %convolution_convert_fusion), channel_id=1, source_target_pairs={{0,0},{473,1},{506,2},{483,3},{4,4},{477,5},{510,6},{487,7},{8,8},... | collective-permute-start | bytes 3145736 | tf_op jit(solution)/shard_map/ppermute | solution.py:97

commit v4 on v1

--- a/solution.py
+++ b/solution.py
@@ -3,7 +3,6 @@
 from jax import lax
 from jax.sharding import PartitionSpec as P
 
-STEPS = 4
 GROUP = 16
 HIGH = lax.Precision.HIGHEST
 
@@ -32,8 +31,15 @@
     return out[: rows.shape[0]] + out[rows.shape[0] :]
 
 
+def project(values, matrix):
+    layers, examples, tokens, width = values.shape
+    halves = values.reshape(layers, examples, 2, tokens // 2, width)
+    part = jnp.einsum("lehsd,ldr->lehrs", halves, matrix, preferred_element_type=jnp.float32)
+    return part.astype(jnp.bfloat16)
+
+
 def shards(activations, out_grads, proj_in, proj_out, lengths, test_feats, test_slot):
-    layers, examples, tokens, _ = activations.shape
+    _, examples, tokens, _ = activations.shape
     rank = proj_in.shape[2]
     block, feats = test_feats.shape[1], test_feats.shape[2]
     half_feats, half_tokens = feats // 2, tokens // 2
@@ -46,16 +52,14 @@
     ordered = jnp.dot(place, piece, preferred_element_type=jnp.float32).astype(jnp.bfloat16)
     test_block = lax.ppermute(ordered, ("dp", "tensor"), block_pairs(lax.axis_size("dp")))
 
-    part_act = jnp.einsum("lesd,ldr->lesr", activations, proj_in, preferred_element_type=jnp.float32)
-    part_grad = jnp.einsum("lesd,ldr->lesr", out_grads, proj_out, preferred_element_type=jnp.float32)
-    part = jnp.concatenate([part_act, part_grad], axis=3).astype(jnp.bfloat16)
-    part = part.reshape(GROUP, half_tokens, 2 * rank)
+    sides = [project(activations, proj_in), project(out_grads, proj_out)]
+    part = jnp.concatenate(sides, axis=3).reshape(GROUP, 2 * rank, half_tokens)
     part = lax.all_to_all(part, "tensor", 0, 0)
     proj = jnp.sum(part.astype(jnp.float32), axis=0)
     position = (k & 1) * half_tokens + jnp.arange(half_tokens, dtype=jnp.int32)
     kept = position < lengths[(k >> 1) & 3]
-    grad = jnp.where(kept[:, None], proj[:, rank:], 0.0)
-    outer = jnp.einsum("sa,sb->ab", grad, proj[:, :rank], precision=HIGH)
+    grad = jnp.where(kept[None, :], proj[rank:], 0.0)
+    outer = jnp.einsum("as,bs->ab", grad, proj[:rank], precision=HIGH)
     outer = outer.reshape(2, 1, rank // 4, 2 * rank)
     outer = jnp.broadcast_to(outer, (2, 4, rank // 4, 2 * rank)).reshape(8, rank // 4, 2 * rank)
     groups = [list(range(8)), list(range(8, 16))]

time: 64.4 us -> 63.7 us (0.989)
  local copies, waits for them, and re-layouts: 3.54 us -> 1.96 us
  other arithmetic: 1.51 us -> 2.33 us
    concatenate x3 -> x0, local copies, waits for them, and re-layouts: 1.16 us -> none  [shards(): part = jnp.concatenate([part_act, part_grad], axis=3).astype(jnp.bfloat16)]
    concatenate x1, other arithmetic: 0.05 us -> 0.86 us  [shards(): part = jnp.concatenate(sides, axis=3).reshape(GROUP, 2 * rank, half_tokens)]
where the time goes in v4:
time: 63.7 us; the launch traced here: 63.2 us
  blocking collectives  25.4 us (40%)
  waiting for transfers between devices  14.2 us (22%)
  starting transfers between devices  12.8 us (20%)
  matrix products  6.45 us (10%)
  other arithmetic  2.33 us (4%)
  local copies, waits for them, and re-layouts  1.96 us (3%)
    all_to_all x1, blocking collectives, shards(): lax.all_to_all(jnp.broadcast_to(scores[None], (GROUP, examples, block)),...  17 us
    all_to_all x1, starting transfers between devices, shards(): part = lax.all_to_all(part, 'tensor', 0, 0)  10.2 us
    ppermute x1, waiting for transfers between devices, shards(): lax.ppermute(ordered, ('dp', 'tensor'), block_pairs(lax.axis_size('dp')))  9.95 us
    all_to_all x1, blocking collectives, shards(): outer = lax.all_to_all(outer, 'tensor', 0, 0, axis_index_groups=groups)  8.47 us
    all_to_all x1, waiting for transfers between devices, shards(): part = lax.all_to_all(part, 'tensor', 0, 0)  4.21 us
    dot_general x2, matrix products, project(): jnp.einsum('lehsd,ldr->lehrs', halves, matrix, preferred_element_type=jnp...  3 us
    ppermute x1, starting transfers between devices, shards(): lax.ppermute(ordered, ('dp', 'tensor'), block_pairs(lax.axis_size('dp')))  2.59 us
    dot_general x1, matrix products, shards(): jnp.dot(place, piece, preferred_element_type=jnp.float32)  1.68 us
  transfers between devices with their start and end apart: 2, of which 2 were waited for; matrix products, arithmetic and copies ran while one was open for 5% of the time, Pallas kernels for 0%

profile of v4, /device:TPU:1, one launch (start us, length us, event | category | flops | bytes accessed | tf_op | source)
XLA Modules:
  0.0 63.2 jit_solution(8637834210585460924)
XLA Ops:
  0.0 0.0 copy-start
  0.0 0.0 copy-start.1
  0.0 1.2 %copy-done = bf16[2,4,256,256]{3,2,1,0:T(8,128)(2,1)S(1)} copy-done((bf16[2,4,256,256]{3,2,1,0:T(8,128)(2,1)S(1)}, bf16[2,4,256,256]{3,2,1,0:T(8,128)(2,1)}, u32[]{:S(2)}) %copy-start) | copy-done | bytes 1048600
  1.2 0.0 copy-start.2
  1.2 1.3 %fusion = bf16[2,4,2,64,128]{4,3,2,1,0:T(8,128)(2,1)S(1)} fusion(bf16[2,4,2,128,256]{4,3,2,1,0:T(8,128)(2,1)S(1)} %bitcast.34, bf16[2,256,64]{1,2,0:T(8,128)(2,1)} %param.9), kind=kOutput, calls=%fused_computation.3 | convolution fusion | flops 67239936 | bytes 1376256 | tf_op jit(solution)/shard_map/lehsd,ldr->lehrs/dot_general | solution.py:37
  2.5 1.7 %fusion.1 = bf16[2,4,2,64,128]{4,3,2,1,0:T(8,128)(2,1)S(1)} fusion(bf16[2,4,2,128,256]{4,3,2,1,0:T(8,128)(2,1)} %bitcast.35, bf16[2,256,64]{1,2,0:T(8,128)(2,1)} %param.10), kind=kOutput, calls=%fused_computation.4 | convolution fusion | flops 67239936 | bytes 1376256 | tf_op jit(solution)/shard_map/lehsd,ldr->lehrs/dot_general | solution.py:37
  4.2 0.9 %pad_maximum_fusion = bf16[2,4,2,128,128]{4,3,2,1,0:T(8,128)(2,1)} fusion(bf16[2,4,2,64,128]{4,3,2,1,0:T(8,128)(2,1)S(1)} %fusion.1, bf16[2,4,2,64,128]{4,3,2,1,0:T(8,128)(2,1)S(1)} %fusion), kind=kLoop, calls=%fused_computation.8 | loop fusion | flops 1048576 | bytes 1048576 | tf_op jit(solution)/shard_map/concatenate | solution.py:56
  5.1 10.2 %all-to-all-start = ((bf16[16,128,128]{2,1,0:T(8,128)(2,1)}), bf16[16,128,128]{2,1,0:T(8,128)(2,1)S(1)}, u32[]{:S(2)}, u32[]{:S(2)}) async-start(bf16[16,128,128]{2,1,0:T(8,128)(2,1)} %bitcast.9), calls=%async_computation | async-start | bytes 1048576 | tf_op jit(solution)/shard_map/all_to_all | solution.py:57
  15.3 0.0 copy-done.1
  15.3 1.7 %convolution_convert_fusion = bf16[256,2048]{1,0:T(8,128)(2,1)S(1)} fusion(bf16[2,256,4096]{2,1,0:T(8,128)(2,1)} %param.12, s32[]{:T(128)S(6)} %select_n.15, s32[]{:T(128)S(6)} %select_n.16, s32[256]{0:T(256)S(1)} %copy-done.1), kind=kOutput, calls=%fused_computation | convolution fusion | flops 269025280 | bytes 2098184 | tf_op jit(solution)/shard_map/dot_general | solution.py:52
  17.0 2.6 %collective-permute-start = (bf16[256,2048]{1,0:T(8,128)(2,1)S(1)}, bf16[256,2048]{1,0:T(8,128)(2,1)}, u32[]{:S(2)}, u32[]{:S(2)}) collective-permute-start(bf16[256,2048]{1,0:T(8,128)(2,1)S(1)} %convolution_convert_fusion), channel_id=1, source_target_pairs={{0,0},{473,1},{506,2},{483,3},{4,4},{477,5},{510,6},{487,7},{8,8},... | collective-permute-start | bytes 3145736 | tf_op jit(solution)/shard_map/ppermute | solution.py:53
  19.6 0.0 copy-done.2
  19.6 0.6 dynamic_slice.6
  20.2 0.7 %add_compare_fusion = pred[128]{0:T(512)(128)(4,1)S(1)} fusion(s32[]{:T(128)} %bitcast, s32[]{:T(128)S(6)} %mul.12), kind=kLoop, calls=%fused_computation.29 | loop fusion | flops 256 | bytes 136 | tf_op jit(solution)/shard_map/lt | solution.py:60
  20.8 4.2 %all-to-all-done = bf16[16,128,128]{2,1,0:T(8,128)(2,1)S(1)} async-done(((bf16[16,128,128]{2,1,0:T(8,128)(2,1)}), bf16[16,128,128]{2,1,0:T(8,128)(2,1)S(1)}, u32[]{:S(2)}, u32[]{:S(2)}) %all-to-all-start) | async-done | bytes 524320 | tf_op jit(solution)/shard_map/all_to_all | solution.py:57
  25.0 0.1 convert_reduce_fusion
  25.1 0.2 fusion.7
  25.3 0.1 broadcast_in_dim.30
  25.4 8.5 %all_to_all.15 = f32[8,16,128]{2,1,0:T(8,128)S(1)} all-to-all(f32[8,16,128]{2,1,0:T(8,128)S(1)} %bitcast.37), channel_id=1, replica_groups={{0,1,2,3,4,5,6,7},{8,9,10,11,12,13,14,15},{16,17,18,19,20,21,22,23},{24..., dimensions={0} | all-to-all | bytes 131072 | tf_op jit(solution)/shard_map/all_to_all | solution.py:66
  33.9 0.1 reduce_sum.28
  34.0 9.9 %collective-permute-done = bf16[256,2048]{1,0:T(8,128)(2,1)} collective-permute-done((bf16[256,2048]{1,0:T(8,128)(2,1)S(1)}, bf16[256,2048]{1,0:T(8,128)(2,1)}, u32[]{:S(2)}, u32[]{:S(2)}) %collective-permute-start) | collective-permute-done | bytes 1048608 | tf_op jit(solution)/shard_map/ppermute | solution.py:53
  44.0 1.6 %fusion.9 = f32[8,256]{1,0:T(8,128)S(1)} fusion(bf16[256,2048]{1,0:T(8,128)(2,1)} %collective-permute-done, bf16[4,2048]{1,0:T(4,128)(2,1)S(1)} %get-tuple-element.5, bf16[4,2048]{1,0:T(4,128)(2,1)S(1)} %get-tuple-element.6), kind=kOutput, calls=%fused_computation.16 | convolution fusion | flops 8454144 | bytes 1089536 | tf_op jit(solution)/shard_map/ef,tf->et/dot_general | solution.py:30
  45.6 17.0 %all_to_all.16 = f32[16,4,256]{2,1,0:T(4,128)S(1)} all-to-all(f32[16,4,256]{2,1,0:T(4,128)S(1)} %broadcast_in_dim.32), channel_id=1, replica_groups=mesh['dp'=32,'tensor'=16] {'tensor'}, dimensions={0} | all-to-all | bytes 131072 | tf_op jit(solution)/shard_map/all_to_all | solution.py:70
  62.6 0.6 pad_maximum_fusion.1
  (7 shorter events, 0.1 us)
Async XLA Ops:
  0.0 1.2 %copy-start = (bf16[2,4,256,256]{3,2,1,0:T(8,128)(2,1)S(1)}, bf16[2,4,256,256]{3,2,1,0:T(8,128)(2,1)}, u32[]{:S(2)}) copy-start(bf16[2,4,256,256]{3,2,1,0:T(8,128)(2,1)} %param.7) | copy-start | bytes 3145732
  0.0 15.3 %copy-start.1 = (s32[256]{0:T(256)S(1)}, s32[256]{0:T(256)}, u32[]{:S(2)}) copy-start(s32[256]{0:T(256)} %param.13) | copy-start | bytes 3076
  1.2 18.4 %copy-start.2 = (s32[4]{0:T(128)S(1)}, s32[4]{0:T(128)}, u32[]{:S(2)}) copy-start(s32[4]{0:T(128)} %param.11) | copy-start | bytes 52
  5.1 20.0 %all-to-all-start = ((bf16[16,128,128]{2,1,0:T(8,128)(2,1)}), bf16[16,128,128]{2,1,0:T(8,128)(2,1)S(1)}, u32[]{:S(2)}, u32[]{:S(2)}) async-start(bf16[16,128,128]{2,1,0:T(8,128)(2,1)} %bitcast.9), calls=%async_computation | async-start | bytes 1048576 | tf_op jit(solution)/shard_map/all_to_all | solution.py:57
  17.0 27.0 %collective-permute-start = (bf16[256,2048]{1,0:T(8,128)(2,1)S(1)}, bf16[256,2048]{1,0:T(8,128)(2,1)}, u32[]{:S(2)}, u32[]{:S(2)}) collective-permute-start(bf16[256,2048]{1,0:T(8,128)(2,1)S(1)} %convolution_convert_fusion), channel_id=1, source_target_pairs={{0,0},{473,1},{506,2},{483,3},{4,4},{477,5},{510,6},{487,7},{8,8},... | collective-permute-start | bytes 3145736 | tf_op jit(solution)/shard_map/ppermute | solution.py:53

commit v5 on v4

v5 whole, which is shorter than its diff:
```python
import jax
import jax.numpy as jnp
from jax import lax
from jax.sharding import PartitionSpec as P

GROUP = 16
HIGH = lax.Precision.HIGHEST
BOTH = ("dp", "tensor")


def index_of(plane, side, layer, y, core, planes):
    return ((plane % planes) * 2 + side) * GROUP + layer * 8 + y * 2 + core


def block_pairs(planes):
    pairs = []
    for plane in range(planes):
        for side in range(2):
            for layer in range(2):
                for y in range(4):
                    for core in range(2):
                        near = side == y // 2
                        if core == 1 and near:
                            continue
                        back, source_side, source_core = (1, 0, 1) if core else (1, 1, 0) if near else (2, 1, 1)
                        source_layer = layer ^ (side != source_side)
                        source = index_of(plane - back, source_side, source_layer, y, source_core, planes)
                        pairs.append((source, index_of(plane, side, layer, y, core, planes)))
    return pairs


def sent_side(side, y, core):
    near = (y >> 1) ^ core
    return jnp.where(side == 1, near, 1 - (y >> 1))


def split_dot(rows, block):
    high = rows.astype(jnp.bfloat16)
    low = (rows - high.astype(jnp.float32)).astype(jnp.bfloat16)
    both = jnp.concatenate([high, low], axis=0)
    out = jnp.einsum("ef,tf->et", both, block, preferred_element_type=jnp.float32)
    return out[: rows.shape[0]] + out[rows.shape[0] :]


def project(values, matrix):
    layers, examples, tokens, width = values.shape
    halves = values.reshape(layers, examples, 2, tokens // 2, width)
    part = jnp.einsum("lehsd,ldr->lehrs", halves, matrix, preferred_element_type=jnp.float32)
    return part.astype(jnp.bfloat16)


def shards(activations, out_grads, proj_in, proj_out, lengths, test_feats, test_slot):
    _, examples, tokens, _ = activations.shape
    rank = proj_in.shape[2]
    block, feats = test_feats.shape[1], test_feats.shape[2]
    half_feats, quarter, half_tokens = feats // 2, feats // 4, tokens // 2
    planes = lax.axis_size("dp") // 2
    k = lax.axis_index("tensor")
    side = lax.axis_index("dp") & 1
    layer, y, core = k >> 3, (k >> 1) & 3, k & 1
    near = side == (y >> 1)

    place = (jnp.arange(block, dtype=jnp.int32)[:, None] == test_slot[None, :]).astype(jnp.bfloat16)

    def ordered(layer, first, width):
        piece = lax.dynamic_slice(test_feats, (layer, 0, first), (1, block, width))[0]
        return jnp.dot(place, piece, preferred_element_type=jnp.float32).astype(jnp.bfloat16)

    moved = ordered(layer ^ side ^ sent_side(side, y, core), y * quarter, quarter)
    moved = lax.ppermute(moved, BOTH, block_pairs(planes))

    sides = [project(activations, proj_in), project(out_grads, proj_out)]
    part = jnp.concatenate(sides, axis=3).reshape(GROUP, 2 * rank, half_tokens)
    part = lax.all_to_all(part, "tensor", 0, 0)
    own = lax.optimization_barrier(ordered(layer, (y & 1) * half_feats, half_feats))
    proj = jnp.sum(part.astype(jnp.float32), axis=0)
    position = core * half_tokens + jnp.arange(half_tokens, dtype=jnp.int32)
    grad = jnp.where((position < lengths[y])[None, :], proj[rank:], 0.0)
    outer = jnp.einsum("as,bs->ab", grad, proj[:rank], precision=HIGH)
    outer = outer.reshape(2, rank // 4, 2 * rank)
    halves = []
    for to_side in range(2):
        for to_y in range(4):
            for to_core in range(2):
                is_own = to_core == 1 and to_side == to_y // 2
                halves.append(outer[to_y % 2 if is_own else to_y // 2])
    groups = [
        [index_of(plane, s, l, t, c, planes) for s in range(2) for t in range(4) for c in range(2)]
        for plane in range(planes)
        for l in range(2)
    ]
    outer = lax.all_to_all(jnp.stack(halves), BOTH, 0, 0, axis_index_groups=groups)
    features = outer.reshape(2 * examples, 2, half_feats).sum(axis=1)
    some = jnp.where((y & 1) == 1, features[:, quarter:], features[:, :quarter])

    from_own = split_dot(features, own)
    scores = jnp.where((core == 1) & near, from_own, split_dot(some, moved))
    scores = jnp.broadcast_to(scores.reshape(2, 1, examples, block), (2, GROUP, examples, block))
    groups = [
        [(plane * 2) * GROUP + place for place in range(2 * GROUP)] for plane in range(planes)
    ]
    scores = lax.all_to_all(
        scores.reshape(2 * GROUP, examples, block), BOTH, 0, 0, axis_index_groups=groups
    )
    got = scores.reshape(2, 2, 4, 2, examples, block).sum(axis=1)
    own_0 = got[0, 0, 1] + got[0, 1, 1]
    own_1 = got[1, 2, 1] + got[1, 3, 1]
    back_1 = got[0, 0, 0] + got[0, 1, 0] + got[1, 2, 0] + got[1, 3, 0]
    back_2 = got[0, 2, 1] + got[0, 3, 1] + got[1, 0, 1] + got[1, 1, 1]
    back_3 = got[0, 2, 0] + got[0, 3, 0] + got[1, 0, 0] + got[1, 1, 0]
    first = jnp.concatenate([own_0, back_1, back_2, back_3], axis=1)
    second = jnp.concatenate([own_1, own_0, back_1, back_2], axis=1)
    return jnp.where(side == 0, first, second)


def solution(mesh):
    return jax.shard_map(
        shards,
        mesh=mesh,
        in_specs=(
            P(None, "dp", None, "tensor"),
            P(None, "dp", None, "tensor"),
            P(None, "tensor", None),
            P(None, "tensor", None),
            P("dp"),
            P(None, "dp", None),
            P("dp"),
        ),
        out_specs=P("dp", None),
        check_vma=False,
    )
```

time: 63.7 us -> 62 us (0.973)
  blocking collectives: 25.4 us -> 0 us
  local copies, waits for them, and re-layouts: 1.96 us -> 12.3 us
  starting transfers between devices: 12.8 us -> 21.5 us
  waiting for transfers between devices: 14.2 us -> 18.3 us
    all_to_all x2 -> x0, blocking collectives: 25.4 us -> none  [the longest x1 17 us: shards(): lax.all_to_all(jnp.broadcast_to(scores[None], (GROUP, examples, block)),...]
    all_to_all x0 -> x2, waiting for transfers between devices: none -> 13.8 us  [the longest x1 7.78 us: shards(): lax.all_to_all(scores.reshape(2 * GROUP, examples, block), BOTH, 0, 0, ax...]
    ppermute x1, waiting for transfers between devices: 9.95 us -> 0.01 us  [shards(): moved = lax.ppermute(moved, BOTH, block_pairs(planes))]
    unnamed x6 -> x21, local copies, waits for them, and re-layouts: 1.23 us -> 10.2 us
    all_to_all x0 -> x2, starting transfers between devices: none -> 8.74 us  [the longest x1 4.56 us: shards(): lax.all_to_all(jnp.stack(halves), BOTH, 0, 0, axis_index_groups=groups)]
    dot_general x1 -> x2, matrix products: 1.68 us -> 3.02 us  [ordered(): jnp.dot(place, piece, preferred_element_type=jnp.float32)]
    dot_general x1 -> x2, matrix products: 1.59 us -> 0.63 us  [split_dot(): jnp.einsum('ef,tf->et', both, block, preferred_element_type=jnp.float32)]
  transfers between devices with their start and end apart: 2 -> 4, of which waited for: 2 -> 3; matrix products, arithmetic and copies ran while one was open for 5% -> 24% of each run, Pallas kernels for 0% -> 0%
where the time goes in v5:
time: 62 us; the launch traced here: 61.5 us
  starting transfers between devices  21.5 us (35%)
  waiting for transfers between devices  18.3 us (30%)
  local copies, waits for them, and re-layouts  12.3 us (20%)
  matrix products  6.82 us (11%)
  other arithmetic  2.41 us (4%)
    all_to_all x1, starting transfers between devices, shards(): part = lax.all_to_all(part, 'tensor', 0, 0)  10.2 us
    unnamed x21, local copies, waits for them, and re-layouts  10.2 us
    all_to_all x1, waiting for transfers between devices, shards(): lax.all_to_all(scores.reshape(2 * GROUP, examples, block), BOTH, 0, 0, ax...  7.78 us
    all_to_all x1, waiting for transfers between devices, shards(): lax.all_to_all(jnp.stack(halves), BOTH, 0, 0, axis_index_groups=groups)  6.02 us
    all_to_all x1, starting transfers between devices, shards(): lax.all_to_all(jnp.stack(halves), BOTH, 0, 0, axis_index_groups=groups)  4.56 us
    all_to_all x1, waiting for transfers between devices, shards(): part = lax.all_to_all(part, 'tensor', 0, 0)  4.51 us
    all_to_all x1, starting transfers between devices, shards(): lax.all_to_all(scores.reshape(2 * GROUP, examples, block), BOTH, 0, 0, ax...  4.18 us
    dot_general x2, matrix products, ordered(): jnp.dot(place, piece, preferred_element_type=jnp.float32)  3.02 us
  transfers between devices with their start and end apart: 4, of which 3 were waited for; matrix products, arithmetic and copies ran while one was open for 24% of the time, Pallas kernels for 0%

profile of v5, /device:TPU:1, one launch (start us, length us, event | category | flops | bytes accessed | tf_op | source)
XLA Modules:
  0.0 61.5 jit_solution(16472837280357994472)
XLA Ops:
  0.0 0.0 copy-start
  0.0 0.0 copy-start.1
  0.0 1.2 %copy-done = bf16[2,4,256,256]{3,2,1,0:T(8,128)(2,1)S(1)} copy-done((bf16[2,4,256,256]{3,2,1,0:T(8,128)(2,1)S(1)}, bf16[2,4,256,256]{3,2,1,0:T(8,128)(2,1)}, u32[]{:S(2)}) %copy-start) | copy-done | bytes 1048600
  1.2 0.0 copy-start.2
  1.2 1.3 %fusion = bf16[2,4,2,64,128]{4,3,2,1,0:T(8,128)(2,1)S(1)} fusion(bf16[2,4,2,128,256]{4,3,2,1,0:T(8,128)(2,1)S(1)} %bitcast.40, bf16[2,256,64]{1,2,0:T(8,128)(2,1)} %param.9), kind=kOutput, calls=%fused_computation.4 | convolution fusion | flops 67239936 | bytes 1376256 | tf_op jit(solution)/shard_map/lehsd,ldr->lehrs/dot_general | solution.py:48
  2.5 1.7 %fusion.1 = bf16[2,4,2,64,128]{4,3,2,1,0:T(8,128)(2,1)S(1)} fusion(bf16[2,4,2,128,256]{4,3,2,1,0:T(8,128)(2,1)} %bitcast.41, bf16[2,256,64]{1,2,0:T(8,128)(2,1)} %param.10), kind=kOutput, calls=%fused_computation.5 | convolution fusion | flops 67239936 | bytes 1376256 | tf_op jit(solution)/shard_map/lehsd,ldr->lehrs/dot_general | solution.py:48
  4.2 0.8 %pad_maximum_fusion = bf16[2,4,2,128,128]{4,3,2,1,0:T(8,128)(2,1)} fusion(bf16[2,4,2,64,128]{4,3,2,1,0:T(8,128)(2,1)S(1)} %fusion.1, bf16[2,4,2,64,128]{4,3,2,1,0:T(8,128)(2,1)S(1)} %fusion), kind=kLoop, calls=%fused_computation.9 | loop fusion | flops 1048576 | bytes 1048576 | tf_op jit(solution)/shard_map/concatenate | solution.py:73
  5.1 10.2 %all-to-all-start = ((bf16[16,128,128]{2,1,0:T(8,128)(2,1)}), bf16[16,128,128]{2,1,0:T(8,128)(2,1)S(1)}, u32[]{:S(2)}, u32[]{:S(2)}) async-start(bf16[16,128,128]{2,1,0:T(8,128)(2,1)} %bitcast.9), calls=%async_computation | async-start | bytes 1048576 | tf_op jit(solution)/shard_map/all_to_all | solution.py:74
  15.3 0.0 copy-done.1
  15.3 1.4 %convolution_convert_fusion.1 = bf16[256,1024]{1,0:T(8,128)(2,1)S(1)} fusion(bf16[2,256,4096]{2,1,0:T(8,128)(2,1)} %param.12, s32[]{:T(128)S(6)} %select_n.56, s32[]{:T(128)S(6)} %select_n.57, s32[256]{0:T(256)S(1)} %copy-done.1), kind=kOutput, calls=%fused_computation.1 | convolution fusion | flops 134545408 | bytes 1049608 | tf_op jit(solution)/shard_map/dot_general | solution.py:67
  16.6 2.6 %collective-permute-start = (bf16[256,1024]{1,0:T(8,128)(2,1)S(1)}, bf16[256,1024]{1,0:T(8,128)(2,1)S(1)}, u32[]{:S(2)}, u32[]{:S(2)}) collective-permute-start(bf16[256,1024]{1,0:T(8,128)(2,1)S(1)} %convolution_convert_fusion.1), channel_id=1, source_target_pairs={{504,0},{506,2},{477,4},{485,5},{479,6},{487,7},{496,8},{498,10},{... | collective-permute-start | bytes 1572872 | tf_op jit(solution)/shard_map/ppermute | solution.py:70
  19.3 0.0 copy-done.2
  19.3 0.6 dynamic_slice.9
  19.9 0.7 %add_compare_fusion = pred[128]{0:T(512)(128)(4,1)S(1)} fusion(s32[]{:T(128)} %bitcast, s32[]{:T(128)S(6)} %mul.9), kind=kLoop, calls=%fused_computation.70 | loop fusion | flops 256 | bytes 136 | tf_op jit(solution)/shard_map/lt | solution.py:78
  20.5 4.5 %all-to-all-done = bf16[16,128,128]{2,1,0:T(8,128)(2,1)S(1)} async-done(((bf16[16,128,128]{2,1,0:T(8,128)(2,1)}), bf16[16,128,128]{2,1,0:T(8,128)(2,1)S(1)}, u32[]{:S(2)}, u32[]{:S(2)}) %all-to-all-start) | async-done | bytes 524320 | tf_op jit(solution)/shard_map/all_to_all | solution.py:74
  25.0 0.1 convert_reduce_fusion
  25.1 0.2 fusion.14
  25.3 0.1 slice.103
  25.4 0.1 slice.101
  25.4 0.6 constant_dynamic-update-slice_fusion.15
  26.0 0.6 constant_dynamic-update-slice_fusion.14
  26.6 0.6 constant_dynamic-update-slice_fusion.13
  27.2 0.6 constant_dynamic-update-slice_fusion.12
  27.8 0.6 constant_dynamic-update-slice_fusion.11
  28.4 0.6 constant_dynamic-update-slice_fusion.10
  29.0 0.6 constant_dynamic-update-slice_fusion.9
  29.6 0.6 constant_dynamic-update-slice_fusion.8
  30.2 0.6 constant_dynamic-update-slice_fusion.7
  30.8 0.6 constant_dynamic-update-slice_fusion.6
  31.4 0.6 constant_dynamic-update-slice_fusion.5
  32.0 0.6 constant_dynamic-update-slice_fusion.4
  32.6 0.6 constant_dynamic-update-slice_fusion.3
  33.2 0.6 constant_dynamic-update-slice_fusion.2
  33.8 0.6 constant_dynamic-update-slice_fusion.1
  34.4 0.6 constant_dynamic-update-slice_fusion
  35.0 4.6 %all-to-all-start.1 = ((f32[16,16,128]{2,1,0:T(8,128)}), f32[16,16,128]{2,1,0:T(8,128)S(1)}, u32[]{:S(2)}, u32[]{:S(2)}) async-start(f32[16,16,128]{2,1,0:T(8,128)} %constant_dynamic-update-slice_fusion), calls=%async_computation.1 | async-start | bytes 262144 | tf_op jit(solution)/shard_map/all_to_all | solution.py:92
  39.5 1.7 %convolution_convert_fusion = bf16[256,2048]{1,0:T(8,128)(2,1)S(1)} fusion(bf16[2,256,4096]{2,1,0:T(8,128)(2,1)} %param.12, s32[]{:T(128)S(6)} %select_n.51, s32[]{:T(128)S(6)} %select_n.52, s32[256]{0:T(256)S(1)} %copy-done.1), kind=kOutput, calls=%fused_computation | convolution fusion | flops 269025280 | bytes 2098184 | tf_op jit(solution)/shard_map/dot_general | solution.py:67
  41.2 6.0 %all-to-all-done.1 = f32[16,16,128]{2,1,0:T(8,128)S(1)} async-done(((f32[16,16,128]{2,1,0:T(8,128)}), f32[16,16,128]{2,1,0:T(8,128)S(1)}, u32[]{:S(2)}, u32[]{:S(2)}) %all-to-all-start.1) | async-done | bytes 131104 | tf_op jit(solution)/shard_map/all_to_all | solution.py:92
  47.2 0.1 reshape.43
  47.3 0.2 reduce_sum.28
  47.5 0.4 fusion.8
  47.9 0.0 collective-permute-done
  47.9 0.3 fusion.16
  48.2 0.7 %broadcast_in_dim.25 = f32[2,16,4,256]{3,2,1,0:T(4,128)} broadcast(f32[2,4,256]{2,1,0:T(4,128)S(1)} %broadcast_in_dim.24), dimensions={0,2,3} | broadcast | bytes 139264 | tf_op jit(solution)/shard_map/broadcast_in_dim | solution.py:98
  48.8 4.2 %all-to-all-start.2 = ((f32[32,4,256]{2,1,0:T(4,128)}), f32[32,4,256]{2,1,0:T(4,128)S(1)}, u32[]{:S(2)}, u32[]{:S(2)}) async-start(f32[32,4,256]{2,1,0:T(4,128)} %bitcast.12), calls=%async_computation.2 | async-start | bytes 262144 | tf_op jit(solution)/shard_map/all_to_all | solution.py:102
  53.0 7.8 %all-to-all-done.2 = f32[32,4,256]{2,1,0:T(4,128)S(1)} async-done(((f32[32,4,256]{2,1,0:T(4,128)}), f32[32,4,256]{2,1,0:T(4,128)S(1)}, u32[]{:S(2)}, u32[]{:S(2)}) %all-to-all-start.2) | async-done | bytes 131104 | tf_op jit(solution)/shard_map/all_to_all | solution.py:102
  60.9 0.6 maximum_select_fusion
  (7 shorter events, 0.1 us)
Async XLA Ops:
  0.0 1.2 %copy-start = (bf16[2,4,256,256]{3,2,1,0:T(8,128)(2,1)S(1)}, bf16[2,4,256,256]{3,2,1,0:T(8,128)(2,1)}, u32[]{:S(2)}) copy-start(bf16[2,4,256,256]{3,2,1,0:T(8,128)(2,1)} %param.7) | copy-start | bytes 3145732
  0.0 15.3 %copy-start.1 = (s32[256]{0:T(256)S(1)}, s32[256]{0:T(256)}, u32[]{:S(2)}) copy-start(s32[256]{0:T(256)} %param.13) | copy-start | bytes 3076
  1.2 18.0 %copy-start.2 = (s32[4]{0:T(128)S(1)}, s32[4]{0:T(128)}, u32[]{:S(2)}) copy-start(s32[4]{0:T(128)} %param.11) | copy-start | bytes 52
  5.1 20.0 %all-to-all-start = ((bf16[16,128,128]{2,1,0:T(8,128)(2,1)}), bf16[16,128,128]{2,1,0:T(8,128)(2,1)S(1)}, u32[]{:S(2)}, u32[]{:S(2)}) async-start(bf16[16,128,128]{2,1,0:T(8,128)(2,1)} %bitcast.9), calls=%async_computation | async-start | bytes 1048576 | tf_op jit(solution)/shard_map/all_to_all | solution.py:74
  16.6 31.3 %collective-permute-start = (bf16[256,1024]{1,0:T(8,128)(2,1)S(1)}, bf16[256,1024]{1,0:T(8,128)(2,1)S(1)}, u32[]{:S(2)}, u32[]{:S(2)}) collective-permute-start(bf16[256,1024]{1,0:T(8,128)(2,1)S(1)} %convolution_convert_fusion.1), channel_id=1, source_target_pairs={{504,0},{506,2},{477,4},{485,5},{479,6},{487,7},{496,8},{498,10},{... | collective-permute-start | bytes 1572872 | tf_op jit(solution)/shard_map/ppermute | solution.py:70
  35.0 12.3 %all-to-all-start.1 = ((f32[16,16,128]{2,1,0:T(8,128)}), f32[16,16,128]{2,1,0:T(8,128)S(1)}, u32[]{:S(2)}, u32[]{:S(2)}) async-start(f32[16,16,128]{2,1,0:T(8,128)} %constant_dynamic-update-slice_fusion), calls=%async_computation.1 | async-start | bytes 262144 | tf_op jit(solution)/shard_map/all_to_all | solution.py:92
  48.8 12.0 %all-to-all-start.2 = ((f32[32,4,256]{2,1,0:T(4,128)}), f32[32,4,256]{2,1,0:T(4,128)S(1)}, u32[]{:S(2)}, u32[]{:S(2)}) async-start(f32[32,4,256]{2,1,0:T(4,128)} %bitcast.12), calls=%async_computation.2 | async-start | bytes 262144 | tf_op jit(solution)/shard_map/all_to_all | solution.py:102

commit v6 on v4

--- a/solution.py
+++ b/solution.py
@@ -31,10 +31,12 @@
     return out[: rows.shape[0]] + out[rows.shape[0] :]
 
 
-def project(values, matrix):
+def project(values, matrix, kept=None):
     layers, examples, tokens, width = values.shape
     halves = values.reshape(layers, examples, 2, tokens // 2, width)
     part = jnp.einsum("lehsd,ldr->lehrs", halves, matrix, preferred_element_type=jnp.float32)
+    if kept is not None:
+        part = jnp.where(kept.reshape(1, examples, 2, 1, tokens // 2), part, 0.0)
     return part.astype(jnp.bfloat16)
 
 
@@ -52,14 +54,12 @@
     ordered = jnp.dot(place, piece, preferred_element_type=jnp.float32).astype(jnp.bfloat16)
     test_block = lax.ppermute(ordered, ("dp", "tensor"), block_pairs(lax.axis_size("dp")))
 
-    sides = [project(activations, proj_in), project(out_grads, proj_out)]
+    kept = jnp.arange(tokens, dtype=jnp.int32)[None, :] < lengths[:, None]
+    sides = [project(activations, proj_in), project(out_grads, proj_out, kept)]
     part = jnp.concatenate(sides, axis=3).reshape(GROUP, 2 * rank, half_tokens)
     part = lax.all_to_all(part, "tensor", 0, 0)
     proj = jnp.sum(part.astype(jnp.float32), axis=0)
-    position = (k & 1) * half_tokens + jnp.arange(half_tokens, dtype=jnp.int32)
-    kept = position < lengths[(k >> 1) & 3]
-    grad = jnp.where(kept[None, :], proj[rank:], 0.0)
-    outer = jnp.einsum("as,bs->ab", grad, proj[:rank], precision=HIGH)
+    outer = jnp.einsum("as,bs->ab", proj[rank:], proj[:rank], precision=HIGH)
     outer = outer.reshape(2, 1, rank // 4, 2 * rank)
     outer = jnp.broadcast_to(outer, (2, 4, rank // 4, 2 * rank)).reshape(8, rank // 4, 2 * rank)
     groups = [list(range(8)), list(range(8, 16))]

time: 63.7 us -> 63.7 us (level)
  local copies, waits for them, and re-layouts: 1.96 us -> 0.56 us
  waiting for transfers between devices: 14.2 us -> 15.4 us
    all_to_all x1, waiting for transfers between devices: 4.21 us -> 5.46 us  [shards(): part = lax.all_to_all(part, 'tensor', 0, 0)]
    unnamed x6 -> x4, local copies, waits for them, and re-layouts: 1.23 us -> 0.42 us
  transfers between devices with their start and end apart: 2 -> 2, of which waited for: 2 -> 2; matrix products, arithmetic and copies ran while one was open for 5% -> 3% of each run, Pallas kernels for 0% -> 0%
where the time goes in v6:
time: 63.7 us; the launch traced here: 63.2 us
  blocking collectives  25.5 us (40%)
  waiting for transfers between devices  15.4 us (24%)
  starting transfers between devices  12.8 us (20%)
  matrix products  6.44 us (10%)
  other arithmetic  2.5 us (4%)
    all_to_all x1, blocking collectives, shards(): lax.all_to_all(jnp.broadcast_to(scores[None], (GROUP, examples, block)),...  17 us
    all_to_all x1, starting transfers between devices, shards(): part = lax.all_to_all(part, 'tensor', 0, 0)  10.2 us
    ppermute x1, waiting for transfers between devices, shards(): lax.ppermute(ordered, ('dp', 'tensor'), block_pairs(lax.axis_size('dp')))  9.93 us
    all_to_all x1, blocking collectives, shards(): outer = lax.all_to_all(outer, 'tensor', 0, 0, axis_index_groups=groups)  8.47 us
    all_to_all x1, waiting for transfers between devices, shards(): part = lax.all_to_all(part, 'tensor', 0, 0)  5.46 us
    dot_general x2, matrix products, project(): jnp.einsum('lehsd,ldr->lehrs', halves, matrix, preferred_element_type=jnp...  2.98 us
    ppermute x1, starting transfers between devices, shards(): lax.ppermute(ordered, ('dp', 'tensor'), block_pairs(lax.axis_size('dp')))  2.59 us
    dot_general x1, matrix products, shards(): jnp.dot(place, piece, preferred_element_type=jnp.float32)  1.68 us
  transfers between devices with their start and end apart: 2, of which 2 were waited for; matrix products, arithmetic and copies ran while one was open for 3% of the time, Pallas kernels for 0%

profile of v6, /device:TPU:1, one launch (start us, length us, event | category | flops | bytes accessed | tf_op | source)
XLA Modules:
  0.0 63.2 jit_solution(13107629833156512639)
XLA Ops:
  0.0 0.0 copy-start
  0.0 0.0 copy-start.1
  0.0 0.8 %broadcast_compare_fusion = pred[4,2,128]{2,1,0:T(4,128)(4,1)S(1)} fusion(s32[2,128]{1,0:T(2,128)S(1)} %multiply_add_fusion, s32[4]{0:T(128)} %param.11), kind=kLoop, calls=%fused_computation.28 | loop fusion | flops 1024 | bytes 2064 | tf_op jit(solution)/shard_map/lt | solution.py:57
  0.8 0.4 copy-done
  1.2 1.3 %fusion.1 = bf16[2,4,2,64,128]{4,3,2,1,0:T(8,128)(2,1)S(1)} fusion(bf16[2,4,2,128,256]{4,3,2,1,0:T(8,128)(2,1)S(1)} %bitcast.33, bf16[2,256,64]{1,2,0:T(8,128)(2,1)} %param.9), kind=kOutput, calls=%fused_computation.4 | convolution fusion | flops 67239936 | bytes 1376256 | tf_op jit(solution)/shard_map/lehsd,ldr->lehrs/dot_general | solution.py:37
  2.5 1.7 %fusion.2 = bf16[2,4,2,64,128]{4,3,2,1,0:T(8,128)(2,1)S(1)} fusion(bf16[2,4,2,128,256]{4,3,2,1,0:T(8,128)(2,1)} %bitcast.34, pred[4,2,128]{2,1,0:T(4,128)(4,1)S(1)} %broadcast_compare_fusion, bf16[2,256,64]{1,2,0:T(8,128)(2,1)} %param.10), kind=kOutput, calls=%fused_computation.5 | convolution fusion | flops 67371008 | bytes 1377280 | tf_op jit(solution)/shard_map/lehsd,ldr->lehrs/dot_general | solution.py:37
  4.2 0.9 %pad_maximum_fusion = bf16[2,4,2,128,128]{4,3,2,1,0:T(8,128)(2,1)} fusion(bf16[2,4,2,64,128]{4,3,2,1,0:T(8,128)(2,1)S(1)} %fusion.2, bf16[2,4,2,64,128]{4,3,2,1,0:T(8,128)(2,1)S(1)} %fusion.1), kind=kLoop, calls=%fused_computation.9 | loop fusion | flops 1048576 | bytes 1048576 | tf_op jit(solution)/shard_map/concatenate | solution.py:59
  5.1 10.2 %all-to-all-start = ((bf16[16,128,128]{2,1,0:T(8,128)(2,1)}), bf16[16,128,128]{2,1,0:T(8,128)(2,1)S(1)}, u32[]{:S(2)}, u32[]{:S(2)}) async-start(bf16[16,128,128]{2,1,0:T(8,128)(2,1)} %bitcast.8), calls=%async_computation | async-start | bytes 1048576 | tf_op jit(solution)/shard_map/all_to_all | solution.py:60
  15.3 0.0 copy-done.1
  15.3 1.7 %convolution_convert_fusion = bf16[256,2048]{1,0:T(8,128)(2,1)S(1)} fusion(bf16[2,256,4096]{2,1,0:T(8,128)(2,1)} %param.12, s32[]{:T(128)S(6)} %select_n.12, s32[]{:T(128)S(6)} %select_n.13, s32[256]{0:T(256)S(1)} %copy-done.1), kind=kOutput, calls=%fused_computation | convolution fusion | flops 269025280 | bytes 2098184 | tf_op jit(solution)/shard_map/dot_general | solution.py:54
  17.0 2.6 %collective-permute-start = (bf16[256,2048]{1,0:T(8,128)(2,1)S(1)}, bf16[256,2048]{1,0:T(8,128)(2,1)}, u32[]{:S(2)}, u32[]{:S(2)}) collective-permute-start(bf16[256,2048]{1,0:T(8,128)(2,1)S(1)} %convolution_convert_fusion), channel_id=1, source_target_pairs={{0,0},{473,1},{506,2},{483,3},{4,4},{477,5},{510,6},{487,7},{8,8},... | collective-permute-start | bytes 3145736 | tf_op jit(solution)/shard_map/ppermute | solution.py:55
  19.6 5.5 %all-to-all-done = bf16[16,128,128]{2,1,0:T(8,128)(2,1)S(1)} async-done(((bf16[16,128,128]{2,1,0:T(8,128)(2,1)}), bf16[16,128,128]{2,1,0:T(8,128)(2,1)S(1)}, u32[]{:S(2)}, u32[]{:S(2)}) %all-to-all-start) | async-done | bytes 524320 | tf_op jit(solution)/shard_map/all_to_all | solution.py:60
  25.0 0.1 convert_reduce_fusion
  25.1 0.2 fusion.8
  25.3 0.1 broadcast_in_dim.31
  25.4 8.5 %all_to_all.15 = f32[8,16,128]{2,1,0:T(8,128)S(1)} all-to-all(f32[8,16,128]{2,1,0:T(8,128)S(1)} %bitcast.36), channel_id=1, replica_groups={{0,1,2,3,4,5,6,7},{8,9,10,11,12,13,14,15},{16,17,18,19,20,21,22,23},{24..., dimensions={0} | all-to-all | bytes 131072 | tf_op jit(solution)/shard_map/all_to_all | solution.py:66
  33.9 0.1 reduce_sum.28
  34.0 9.9 %collective-permute-done = bf16[256,2048]{1,0:T(8,128)(2,1)} collective-permute-done((bf16[256,2048]{1,0:T(8,128)(2,1)S(1)}, bf16[256,2048]{1,0:T(8,128)(2,1)}, u32[]{:S(2)}, u32[]{:S(2)}) %collective-permute-start) | collective-permute-done | bytes 1048608 | tf_op jit(solution)/shard_map/ppermute | solution.py:55
  43.9 1.6 %fusion.11 = f32[8,256]{1,0:T(8,128)S(1)} fusion(bf16[256,2048]{1,0:T(8,128)(2,1)} %collective-permute-done, bf16[4,2048]{1,0:T(4,128)(2,1)S(1)} %get-tuple-element.5, bf16[4,2048]{1,0:T(4,128)(2,1)S(1)} %get-tuple-element.6), kind=kOutput, calls=%fused_computation.17 | convolution fusion | flops 8454144 | bytes 1089536 | tf_op jit(solution)/shard_map/ef,tf->et/dot_general | solution.py:30
  45.6 17.0 %all_to_all.16 = f32[16,4,256]{2,1,0:T(4,128)S(1)} all-to-all(f32[16,4,256]{2,1,0:T(4,128)S(1)} %broadcast_in_dim.33), channel_id=1, replica_groups=mesh['dp'=32,'tensor'=16] {'tensor'}, dimensions={0} | all-to-all | bytes 131072 | tf_op jit(solution)/shard_map/all_to_all | solution.py:70
  62.6 0.6 pad_maximum_fusion.1
  (8 shorter events, 0.1 us)
Async XLA Ops:
  0.0 1.2 %copy-start = (bf16[2,4,256,256]{3,2,1,0:T(8,128)(2,1)S(1)}, bf16[2,4,256,256]{3,2,1,0:T(8,128)(2,1)}, u32[]{:S(2)}) copy-start(bf16[2,4,256,256]{3,2,1,0:T(8,128)(2,1)} %param.7) | copy-start | bytes 3145732
  0.0 15.3 %copy-start.1 = (s32[256]{0:T(256)S(1)}, s32[256]{0:T(256)}, u32[]{:S(2)}) copy-start(s32[256]{0:T(256)} %param.13) | copy-start | bytes 3076
  5.1 20.0 %all-to-all-start = ((bf16[16,128,128]{2,1,0:T(8,128)(2,1)}), bf16[16,128,128]{2,1,0:T(8,128)(2,1)S(1)}, u32[]{:S(2)}, u32[]{:S(2)}) async-start(bf16[16,128,128]{2,1,0:T(8,128)(2,1)} %bitcast.8), calls=%async_computation | async-start | bytes 1048576 | tf_op jit(solution)/shard_map/all_to_all | solution.py:60
  17.0 27.0 %collective-permute-start = (bf16[256,2048]{1,0:T(8,128)(2,1)S(1)}, bf16[256,2048]{1,0:T(8,128)(2,1)}, u32[]{:S(2)}, u32[]{:S(2)}) collective-permute-start(bf16[256,2048]{1,0:T(8,128)(2,1)S(1)} %convolution_convert_fusion), channel_id=1, source_target_pairs={{0,0},{473,1},{506,2},{483,3},{4,4},{477,5},{510,6},{487,7},{8,8},... | collective-permute-start | bytes 3145736 | tf_op jit(solution)/shard_map/ppermute | solution.py:55

commit v7 on v6

v7 whole, which is shorter than its diff:
```python
import jax
import jax.numpy as jnp
from jax import lax
from jax.sharding import PartitionSpec as P

GROUP = 16
HIGH = lax.Precision.HIGHEST
BOTH = ("dp", "tensor")


def block_pairs(shard_count, tiles):
    return [
        (shard * GROUP + k, ((shard + tiles[k & 1]) % shard_count) * GROUP + k)
        for shard in range(shard_count)
        for k in range(GROUP)
    ]


def split_dot(rows, block):
    high = rows.astype(jnp.bfloat16)
    low = (rows - high.astype(jnp.float32)).astype(jnp.bfloat16)
    both = jnp.concatenate([high, low], axis=0)
    out = jnp.einsum("ef,tf->et", both, block, preferred_element_type=jnp.float32)
    return out[: rows.shape[0]] + out[rows.shape[0] :]


def project(values, matrix, kept=None):
    layers, examples, tokens, width = values.shape
    halves = values.reshape(layers, examples, 2, tokens // 2, width)
    part = jnp.einsum("lehsd,ldr->lehrs", halves, matrix, preferred_element_type=jnp.float32)
    if kept is not None:
        part = jnp.where(kept.reshape(1, examples, 2, 1, tokens // 2), part, 0.0)
    return part.astype(jnp.bfloat16)


def shards(activations, out_grads, proj_in, proj_out, lengths, test_feats, test_slot):
    _, examples, tokens, _ = activations.shape
    rank = proj_in.shape[2]
    block, quarter = test_feats.shape[1], test_feats.shape[2] // 4
    half_tokens = tokens // 2
    shard_count = lax.axis_size("dp")
    k = lax.axis_index("tensor")

    start = (k >> 3, 0, ((k >> 1) & 3) * quarter)
    piece = lax.dynamic_slice(test_feats, start, (1, block, quarter))[0]
    place = (jnp.arange(block, dtype=jnp.int32)[:, None] == test_slot[None, :]).astype(jnp.bfloat16)
    ordered = jnp.dot(place, piece, preferred_element_type=jnp.float32).astype(jnp.bfloat16)
    odd_block = lax.ppermute(ordered, BOTH, block_pairs(shard_count, (1, 3)))
    even_block = lax.ppermute(ordered, BOTH, block_pairs(shard_count, (2, 0)))

    kept = jnp.arange(tokens, dtype=jnp.int32)[None, :] < lengths[:, None]
    sides = [project(activations, proj_in), project(out_grads, proj_out, kept)]
    part = jnp.concatenate(sides, axis=3).reshape(GROUP, 2 * rank, half_tokens)
    part = lax.all_to_all(part, "tensor", 0, 0)
    proj = jnp.sum(part.astype(jnp.float32), axis=0)
    outer = jnp.einsum("as,bs->ab", proj[rank:], proj[:rank], precision=HIGH)
    outer = outer.reshape(4, 1, rank // 8, 2 * rank)
    outer = jnp.broadcast_to(outer, (4, 2, rank // 8, 2 * rank)).reshape(8, rank // 8, 2 * rank)
    groups = [list(range(8)), list(range(8, 16))]
    outer = lax.all_to_all(outer, "tensor", 0, 0, axis_index_groups=groups)
    features = outer.reshape(examples, 2, quarter).sum(axis=1)

    scores = jnp.concatenate([split_dot(features, odd_block), split_dot(features, even_block)], axis=0)
    scores = jnp.broadcast_to(scores[None], (GROUP, 2 * examples, block))
    scores = lax.all_to_all(scores, "tensor", 0, 0)
    scores = scores.reshape(GROUP // 2, 2, 2, examples, block).sum(axis=0)
    return jnp.concatenate([scores[1, 1], scores[0, 0], scores[0, 1], scores[1, 0]], axis=1)


def solution(mesh):
    return jax.shard_map(
        shards,
        mesh=mesh,
        in_specs=(
            P(None, "dp", None, "tensor"),
            P(None, "dp", None, "tensor"),
            P(None, "tensor", None),
            P(None, "tensor", None),
            P("dp"),
            P(None, "dp", None),
            P("dp"),
        ),
        out_specs=P("dp", None),
        check_vma=False,
    )
```

time: 63.7 us -> 70.7 us (1.11)
  waiting for transfers between devices: 15.4 us -> 30 us
  blocking collectives: 25.5 us -> 13.7 us
  starting transfers between devices: 12.8 us -> 17.7 us
  matrix products: 6.44 us -> 4.99 us
    all_to_all x2 -> x1, blocking collectives: 25.5 us -> 13.7 us  [shards(): scores = lax.all_to_all(scores, 'tensor', 0, 0)]
    ppermute x1 -> x2, waiting for transfers between devices: 9.93 us -> 19.9 us  [the longest x1 19.9 us: shards(): odd_block = lax.ppermute(ordered, BOTH, block_pairs(shard_count, (1, 3)))]
    all_to_all x0 -> x1, starting transfers between devices: none -> 4.48 us  [shards(): outer = lax.all_to_all(outer, 'tensor', 0, 0, axis_index_groups=groups)]
    all_to_all x0 -> x1, waiting for transfers between devices: none -> 2.41 us  [shards(): outer = lax.all_to_all(outer, 'tensor', 0, 0, axis_index_groups=groups)]
    all_to_all x1, waiting for transfers between devices: 5.46 us -> 7.68 us  [shards(): part = lax.all_to_all(part, 'tensor', 0, 0)]
    dot_general x1 -> x2, matrix products: 1.59 us -> 0.47 us  [split_dot(): jnp.einsum('ef,tf->et', both, block, preferred_element_type=jnp.float32)]
    ppermute x1 -> x2, starting transfers between devices: 2.59 us -> 3.01 us  [the longest x1 2.32 us: shards(): odd_block = lax.ppermute(ordered, BOTH, block_pairs(shard_count, (1, 3)))]
  transfers between devices with their start and end apart: 2 -> 4, of which waited for: 2 -> 3; matrix products, arithmetic and copies ran while one was open for 3% -> 4% of each run, Pallas kernels for 0% -> 0%
where the time goes in v7:
time: 70.7 us; the launch traced here: 70.2 us
  waiting for transfers between devices  30 us (42%)
  starting transfers between devices  17.7 us (25%)
  blocking collectives  13.7 us (19%)
  matrix products  4.99 us (7%)
  other arithmetic  2.46 us (3%)
  local copies, waits for them, and re-layouts  1.17 us (2%)
    ppermute x1, waiting for transfers between devices, shards(): odd_block = lax.ppermute(ordered, BOTH, block_pairs(shard_count, (1, 3)))  19.9 us
    all_to_all x1, blocking collectives, shards(): scores = lax.all_to_all(scores, 'tensor', 0, 0)  13.7 us
    all_to_all x1, starting transfers between devices, shards(): part = lax.all_to_all(part, 'tensor', 0, 0)  10.2 us
    all_to_all x1, waiting for transfers between devices, shards(): part = lax.all_to_all(part, 'tensor', 0, 0)  7.68 us
    all_to_all x1, starting transfers between devices, shards(): outer = lax.all_to_all(outer, 'tensor', 0, 0, axis_index_groups=groups)  4.48 us
    dot_general x2, matrix products, project(): jnp.einsum('lehsd,ldr->lehrs', halves, matrix, preferred_element_type=jnp...  2.98 us
    all_to_all x1, waiting for transfers between devices, shards(): outer = lax.all_to_all(outer, 'tensor', 0, 0, axis_index_groups=groups)  2.41 us
    ppermute x1, starting transfers between devices, shards(): odd_block = lax.ppermute(ordered, BOTH, block_pairs(shard_count, (1, 3)))  2.32 us
  transfers between devices with their start and end apart: 4, of which 3 were waited for; matrix products, arithmetic and copies ran while one was open for 4% of the time, Pallas kernels for 0%

profile of v7, /device:TPU:1, one launch (start us, length us, event | category | flops | bytes accessed | tf_op | source)
XLA Modules:
  0.0 70.2 jit_solution(8529883032936156425)
XLA Ops:
  0.0 0.0 copy-start
  0.0 0.0 copy-start.1
  0.0 0.8 %broadcast_compare_fusion = pred[4,2,128]{2,1,0:T(4,128)(4,1)S(1)} fusion(s32[2,128]{1,0:T(2,128)S(1)} %multiply_add_fusion, s32[4]{0:T(128)} %param.11), kind=kLoop, calls=%fused_computation.29 | loop fusion | flops 1024 | bytes 2064 | tf_op jit(solution)/shard_map/lt | solution.py:51
  0.8 0.4 copy-done
  1.2 1.3 %fusion.1 = bf16[2,4,2,64,128]{4,3,2,1,0:T(8,128)(2,1)S(1)} fusion(bf16[2,4,2,128,256]{4,3,2,1,0:T(8,128)(2,1)S(1)} %bitcast.33, bf16[2,256,64]{1,2,0:T(8,128)(2,1)} %param.9), kind=kOutput, calls=%fused_computation.4 | convolution fusion | flops 67239936 | bytes 1376256 | tf_op jit(solution)/shard_map/lehsd,ldr->lehrs/dot_general | solution.py:30
  2.5 1.7 %fusion.2 = bf16[2,4,2,64,128]{4,3,2,1,0:T(8,128)(2,1)S(1)} fusion(bf16[2,4,2,128,256]{4,3,2,1,0:T(8,128)(2,1)} %bitcast.34, pred[4,2,128]{2,1,0:T(4,128)(4,1)S(1)} %broadcast_compare_fusion, bf16[2,256,64]{1,2,0:T(8,128)(2,1)} %param.10), kind=kOutput, calls=%fused_computation.5 | convolution fusion | flops 67371008 | bytes 1377280 | tf_op jit(solution)/shard_map/lehsd,ldr->lehrs/dot_general | solution.py:30
  4.2 0.8 %pad_maximum_fusion = bf16[2,4,2,128,128]{4,3,2,1,0:T(8,128)(2,1)} fusion(bf16[2,4,2,64,128]{4,3,2,1,0:T(8,128)(2,1)S(1)} %fusion.2, bf16[2,4,2,64,128]{4,3,2,1,0:T(8,128)(2,1)S(1)} %fusion.1), kind=kLoop, calls=%fused_computation.7 | loop fusion | flops 1048576 | bytes 1048576 | tf_op jit(solution)/shard_map/concatenate | solution.py:53
  5.1 10.2 %all-to-all-start = ((bf16[16,128,128]{2,1,0:T(8,128)(2,1)}), bf16[16,128,128]{2,1,0:T(8,128)(2,1)S(1)}, u32[]{:S(2)}, u32[]{:S(2)}) async-start(bf16[16,128,128]{2,1,0:T(8,128)(2,1)} %bitcast.8), calls=%async_computation | async-start | bytes 1048576 | tf_op jit(solution)/shard_map/all_to_all | solution.py:54
  15.3 0.0 copy-done.1
  15.3 1.4 %convolution_convert_fusion = bf16[256,1024]{1,0:T(8,128)(2,1)S(1)} fusion(bf16[2,256,4096]{2,1,0:T(8,128)(2,1)} %param.12, s32[]{:T(128)S(6)} %select_n.12, s32[]{:T(128)S(6)} %select_n.13, s32[256]{0:T(256)S(1)} %copy-done.1), kind=kOutput, calls=%fused_computation | convolution fusion | flops 134545408 | bytes 1049608 | tf_op jit(solution)/shard_map/dot_general | solution.py:47
  16.6 0.7 collective-permute-start.1
  17.3 7.7 %all-to-all-done = bf16[16,128,128]{2,1,0:T(8,128)(2,1)S(1)} async-done(((bf16[16,128,128]{2,1,0:T(8,128)(2,1)}), bf16[16,128,128]{2,1,0:T(8,128)(2,1)S(1)}, u32[]{:S(2)}, u32[]{:S(2)}) %all-to-all-start) | async-done | bytes 524320 | tf_op jit(solution)/shard_map/all_to_all | solution.py:54
  25.0 0.1 convert_reduce_fusion
  25.1 0.2 fusion.8
  25.3 0.1 broadcast_in_dim.31
  25.3 0.6 broadcast_in_dim.32
  26.0 4.5 %all-to-all-start.1 = ((f32[8,8,128]{2,1,0:T(8,128)}), f32[8,8,128]{2,1,0:T(8,128)S(1)}, u32[]{:S(2)}, u32[]{:S(2)}) async-start(f32[8,8,128]{2,1,0:T(8,128)} %bitcast.9), calls=%async_computation.1 | async-start | bytes 65536 | tf_op jit(solution)/shard_map/all_to_all | solution.py:60
  30.4 2.3 %collective-permute-start = (bf16[256,1024]{1,0:T(8,128)(2,1)S(1)}, bf16[256,1024]{1,0:T(8,128)(2,1)S(1)}, u32[]{:S(2)}, u32[]{:S(2)}) collective-permute-start(bf16[256,1024]{1,0:T(8,128)(2,1)S(1)} %convolution_convert_fusion), channel_id=1, source_target_pairs={{0,16},{1,49},{2,18},{3,51},{4,20},{5,53},{6,22},{7,55},{8,24},{9,... | collective-permute-start | bytes 1572872 | tf_op jit(solution)/shard_map/ppermute | solution.py:48
  32.8 2.4 %all-to-all-done.1 = f32[8,8,128]{2,1,0:T(8,128)S(1)} async-done(((f32[8,8,128]{2,1,0:T(8,128)}), f32[8,8,128]{2,1,0:T(8,128)S(1)}, u32[]{:S(2)}, u32[]{:S(2)}) %all-to-all-start.1) | async-done | bytes 32800 | tf_op jit(solution)/shard_map/all_to_all | solution.py:60
  35.3 0.0 collective-permute-done.1
  35.3 0.2 fusion.11
  35.5 19.9 %collective-permute-done = bf16[256,1024]{1,0:T(8,128)(2,1)S(1)} collective-permute-done((bf16[256,1024]{1,0:T(8,128)(2,1)S(1)}, bf16[256,1024]{1,0:T(8,128)(2,1)S(1)}, u32[]{:S(2)}, u32[]{:S(2)}) %collective-permute-start) | collective-permute-done | bytes 524320 | tf_op jit(solution)/shard_map/ppermute | solution.py:48
  55.4 0.2 fusion.12
  55.7 13.7 %all_to_all.15 = f32[16,8,256]{2,1,0:T(8,128)S(1)} all-to-all(f32[16,8,256]{2,1,0:T(8,128)S(1)} %broadcast_in_dim.33), channel_id=1, replica_groups=mesh['dp'=32,'tensor'=16] {'tensor'}, dimensions={0} | all-to-all | bytes 262144 | tf_op jit(solution)/shard_map/all_to_all | solution.py:65
  69.6 0.6 pad_maximum_fusion.2
  (11 shorter events, 0.2 us)
Async XLA Ops:
  0.0 1.2 %copy-start = (bf16[2,4,256,256]{3,2,1,0:T(8,128)(2,1)S(1)}, bf16[2,4,256,256]{3,2,1,0:T(8,128)(2,1)}, u32[]{:S(2)}) copy-start(bf16[2,4,256,256]{3,2,1,0:T(8,128)(2,1)} %param.7) | copy-start | bytes 3145732
  0.0 15.2 %copy-start.1 = (s32[256]{0:T(256)S(1)}, s32[256]{0:T(256)}, u32[]{:S(2)}) copy-start(s32[256]{0:T(256)} %param.13) | copy-start | bytes 3076
  5.1 20.0 %all-to-all-start = ((bf16[16,128,128]{2,1,0:T(8,128)(2,1)}), bf16[16,128,128]{2,1,0:T(8,128)(2,1)S(1)}, u32[]{:S(2)}, u32[]{:S(2)}) async-start(bf16[16,128,128]{2,1,0:T(8,128)(2,1)} %bitcast.8), calls=%async_computation | async-start | bytes 1048576 | tf_op jit(solution)/shard_map/all_to_all | solution.py:54
  16.6 18.7 %collective-permute-start.1 = (bf16[256,1024]{1,0:T(8,128)(2,1)S(1)}, bf16[256,1024]{1,0:T(8,128)(2,1)S(1)}, u32[]{:S(2)}, u32[]{:S(2)}) collective-permute-start(bf16[256,1024]{1,0:T(8,128)(2,1)S(1)} %convolution_convert_fusion), channel_id=1, source_target_pairs={{0,32},{1,1},{2,34},{3,3},{4,36},{5,5},{6,38},{7,7},{8,40},{9,9},{... | collective-permute-start | bytes 1572872 | tf_op jit(solution)/shard_map/ppermute | solution.py:49
  26.0 9.2 %all-to-all-start.1 = ((f32[8,8,128]{2,1,0:T(8,128)}), f32[8,8,128]{2,1,0:T(8,128)S(1)}, u32[]{:S(2)}, u32[]{:S(2)}) async-start(f32[8,8,128]{2,1,0:T(8,128)} %bitcast.9), calls=%async_computation.1 | async-start | bytes 65536 | tf_op jit(solution)/shard_map/all_to_all | solution.py:60
  30.4 25.0 %collective-permute-start = (bf16[256,1024]{1,0:T(8,128)(2,1)S(1)}, bf16[256,1024]{1,0:T(8,128)(2,1)S(1)}, u32[]{:S(2)}, u32[]{:S(2)}) collective-permute-start(bf16[256,1024]{1,0:T(8,128)(2,1)S(1)} %convolution_convert_fusion), channel_id=1, source_target_pairs={{0,16},{1,49},{2,18},{3,51},{4,20},{5,53},{6,22},{7,55},{8,24},{9,... | collective-permute-start | bytes 1572872 | tf_op jit(solution)/shard_map/ppermute | solution.py:48

commit v8 on v7

--- a/solution.py
+++ b/solution.py
@@ -10,7 +10,7 @@
 
 def block_pairs(shard_count, tiles):
     return [
-        (shard * GROUP + k, ((shard + tiles[k & 1]) % shard_count) * GROUP + k)
+        (shard * GROUP + k, ((shard + tiles[k & 1]) % shard_count) * GROUP + (k ^ (8 * (tiles[k & 1] & 1))))
         for shard in range(shard_count)
         for k in range(GROUP)
     ]
@@ -45,6 +45,8 @@
     piece = lax.dynamic_slice(test_feats, start, (1, block, quarter))[0]
     place = (jnp.arange(block, dtype=jnp.int32)[:, None] == test_slot[None, :]).astype(jnp.bfloat16)
     ordered = jnp.dot(place, piece, preferred_element_type=jnp.float32).astype(jnp.bfloat16)
+    layer_one = jnp.broadcast_to((k >> 3).astype(jnp.float32), (examples, block))
+    ordered, layer_one = lax.optimization_barrier((ordered, layer_one))
     odd_block = lax.ppermute(ordered, BOTH, block_pairs(shard_count, (1, 3)))
     even_block = lax.ppermute(ordered, BOTH, block_pairs(shard_count, (2, 0)))
 
@@ -54,13 +56,17 @@
     part = lax.all_to_all(part, "tensor", 0, 0)
     proj = jnp.sum(part.astype(jnp.float32), axis=0)
     outer = jnp.einsum("as,bs->ab", proj[rank:], proj[:rank], precision=HIGH)
-    outer = outer.reshape(4, 1, rank // 8, 2 * rank)
-    outer = jnp.broadcast_to(outer, (4, 2, rank // 8, 2 * rank)).reshape(8, rank // 8, 2 * rank)
-    groups = [list(range(8)), list(range(8, 16))]
-    outer = lax.all_to_all(outer, "tensor", 0, 0, axis_index_groups=groups)
-    features = outer.reshape(examples, 2, quarter).sum(axis=1)
+    outer = outer.reshape(1, 4, 1, rank // 8, 2 * rank)
+    outer = jnp.broadcast_to(outer, (2, 4, 2, rank // 8, 2 * rank)).reshape(GROUP, rank // 8, 2 * rank)
+    outer = lax.all_to_all(outer, "tensor", 0, 0)
+    features = outer.reshape(2 * examples, 2, quarter).sum(axis=1)
 
-    scores = jnp.concatenate([split_dot(features, odd_block), split_dot(features, even_block)], axis=0)
+    odd = split_dot(features, odd_block).reshape(2, examples, block)
+    even = split_dot(features, even_block).reshape(2, examples, block)
+    swap = layer_one > 0.5
+    odd = jnp.where(swap, odd[0], odd[1])
+    even = jnp.where(swap, even[1], even[0])
+    scores = jnp.concatenate([odd, even], axis=0)
     scores = jnp.broadcast_to(scores[None], (GROUP, 2 * examples, block))
     scores = lax.all_to_all(scores, "tensor", 0, 0)
     scores = scores.reshape(GROUP // 2, 2, 2, examples, block).sum(axis=0)

time: 70.7 us -> 70.8 us (level)
  blocking collectives: 13.7 us -> 12.7 us
  waiting for transfers between devices: 30 us -> 30.9 us
    all_to_all x1, blocking collectives: 13.7 us -> 12.7 us  [shards(): scores = lax.all_to_all(scores, 'tensor', 0, 0)]
    all_to_all x1, waiting for transfers between devices: 2.41 us -> 3.35 us  [shards(): outer = lax.all_to_all(outer, 'tensor', 0, 0)]
where the time goes in v8:
time: 70.8 us; the launch traced here: 70.3 us
  waiting for transfers between devices  30.9 us (44%)
  starting transfers between devices  18 us (25%)
  blocking collectives  12.7 us (18%)
  matrix products  4.99 us (7%)
  other arithmetic  2.51 us (4%)
  local copies, waits for them, and re-layouts  1.2 us (2%)
    ppermute x1, waiting for transfers between devices, shards(): odd_block = lax.ppermute(ordered, BOTH, block_pairs(shard_count, (1, 3)))  19.9 us
    all_to_all x1, blocking collectives, shards(): scores = lax.all_to_all(scores, 'tensor', 0, 0)  12.7 us
    all_to_all x1, starting transfers between devices, shards(): part = lax.all_to_all(part, 'tensor', 0, 0)  10.2 us
    all_to_all x1, waiting for transfers between devices, shards(): part = lax.all_to_all(part, 'tensor', 0, 0)  7.68 us
    all_to_all x1, starting transfers between devices, shards(): outer = lax.all_to_all(outer, 'tensor', 0, 0)  4.54 us
    all_to_all x1, waiting for transfers between devices, shards(): outer = lax.all_to_all(outer, 'tensor', 0, 0)  3.35 us
    dot_general x2, matrix products, project(): jnp.einsum('lehsd,ldr->lehrs', halves, matrix, preferred_element_type=jnp...  2.98 us
    ppermute x1, starting transfers between devices, shards(): odd_block = lax.ppermute(ordered, BOTH, block_pairs(shard_count, (1, 3)))  2.54 us
  transfers between devices with their start and end apart: 4, of which 3 were waited for; matrix products, arithmetic and copies ran while one was open for 4% of the time, Pallas kernels for 0%

profile of v8, /device:TPU:1, one launch (start us, length us, event | category | flops | bytes accessed | tf_op | source)
XLA Modules:
  0.0 70.3 jit_solution(9623139981459842645)
XLA Ops:
  0.0 0.0 copy-start
  0.0 0.0 copy-start.1
  0.0 0.8 %broadcast_compare_fusion = pred[4,2,128]{2,1,0:T(4,128)(4,1)S(1)} fusion(s32[2,128]{1,0:T(2,128)S(1)} %multiply_add_fusion, s32[4]{0:T(128)} %param.11), kind=kLoop, calls=%fused_computation.31 | loop fusion | flops 1024 | bytes 2064 | tf_op jit(solution)/shard_map/lt | solution.py:53
  0.8 0.4 copy-done
  1.2 1.3 %fusion.1 = bf16[2,4,2,64,128]{4,3,2,1,0:T(8,128)(2,1)S(1)} fusion(bf16[2,4,2,128,256]{4,3,2,1,0:T(8,128)(2,1)S(1)} %bitcast.33, bf16[2,256,64]{1,2,0:T(8,128)(2,1)} %param.9), kind=kOutput, calls=%fused_computation.4 | convolution fusion | flops 67239936 | bytes 1376256 | tf_op jit(solution)/shard_map/lehsd,ldr->lehrs/dot_general | solution.py:30
  2.5 1.7 %fusion.2 = bf16[2,4,2,64,128]{4,3,2,1,0:T(8,128)(2,1)S(1)} fusion(bf16[2,4,2,128,256]{4,3,2,1,0:T(8,128)(2,1)} %bitcast.34, pred[4,2,128]{2,1,0:T(4,128)(4,1)S(1)} %broadcast_compare_fusion, bf16[2,256,64]{1,2,0:T(8,128)(2,1)} %param.10), kind=kOutput, calls=%fused_computation.5 | convolution fusion | flops 67371008 | bytes 1377280 | tf_op jit(solution)/shard_map/lehsd,ldr->lehrs/dot_general | solution.py:30
  4.2 0.8 %pad_maximum_fusion = bf16[2,4,2,128,128]{4,3,2,1,0:T(8,128)(2,1)} fusion(bf16[2,4,2,64,128]{4,3,2,1,0:T(8,128)(2,1)S(1)} %fusion.2, bf16[2,4,2,64,128]{4,3,2,1,0:T(8,128)(2,1)S(1)} %fusion.1), kind=kLoop, calls=%fused_computation.7 | loop fusion | flops 1048576 | bytes 1048576 | tf_op jit(solution)/shard_map/concatenate | solution.py:55
  5.1 10.2 %all-to-all-start = ((bf16[16,128,128]{2,1,0:T(8,128)(2,1)}), bf16[16,128,128]{2,1,0:T(8,128)(2,1)S(1)}, u32[]{:S(2)}, u32[]{:S(2)}) async-start(bf16[16,128,128]{2,1,0:T(8,128)(2,1)} %bitcast.9), calls=%async_computation | async-start | bytes 1048576 | tf_op jit(solution)/shard_map/all_to_all | solution.py:56
  15.3 0.0 copy-done.1
  15.3 1.4 %convolution_convert_fusion = bf16[256,1024]{1,0:T(8,128)(2,1)S(1)} fusion(bf16[2,256,4096]{2,1,0:T(8,128)(2,1)} %param.12, s32[]{:T(128)S(6)} %select_n.18, s32[]{:T(128)S(6)} %select_n.19, s32[256]{0:T(256)S(1)} %copy-done.1), kind=kOutput, calls=%fused_computation | convolution fusion | flops 134545408 | bytes 1049608 | tf_op jit(solution)/shard_map/dot_general | solution.py:47
  16.6 0.7 collective-permute-start.1
  17.3 7.7 %all-to-all-done = bf16[16,128,128]{2,1,0:T(8,128)(2,1)S(1)} async-done(((bf16[16,128,128]{2,1,0:T(8,128)(2,1)}), bf16[16,128,128]{2,1,0:T(8,128)(2,1)S(1)}, u32[]{:S(2)}, u32[]{:S(2)}) %all-to-all-start) | async-done | bytes 524320 | tf_op jit(solution)/shard_map/all_to_all | solution.py:56
  25.0 0.1 convert_reduce_fusion
  25.1 0.2 fusion.8
  25.3 0.1 broadcast_in_dim.35
  25.4 0.6 broadcast_in_dim.36
  26.0 4.5 %all-to-all-start.1 = ((f32[16,8,128]{2,1,0:T(8,128)}), f32[16,8,128]{2,1,0:T(8,128)S(1)}, u32[]{:S(2)}, u32[]{:S(2)}) async-start(f32[16,8,128]{2,1,0:T(8,128)} %bitcast.10), calls=%async_computation.1 | async-start | bytes 131072 | tf_op jit(solution)/shard_map/all_to_all | solution.py:61
  30.5 2.5 %collective-permute-start = (bf16[256,1024]{1,0:T(8,128)(2,1)S(1)}, bf16[256,1024]{1,0:T(8,128)(2,1)S(1)}, u32[]{:S(2)}, u32[]{:S(2)}) collective-permute-start(bf16[256,1024]{1,0:T(8,128)(2,1)S(1)} %convolution_convert_fusion), channel_id=1, source_target_pairs={{0,24},{1,57},{2,26},{3,59},{4,28},{5,61},{6,30},{7,63},{8,16},{9,... | collective-permute-start | bytes 1572872 | tf_op jit(solution)/shard_map/ppermute | solution.py:50
  33.1 3.3 %all-to-all-done.1 = f32[16,8,128]{2,1,0:T(8,128)S(1)} async-done(((f32[16,8,128]{2,1,0:T(8,128)}), f32[16,8,128]{2,1,0:T(8,128)S(1)}, u32[]{:S(2)}, u32[]{:S(2)}) %all-to-all-start.1) | async-done | bytes 65568 | tf_op jit(solution)/shard_map/all_to_all | solution.py:61
  36.5 0.1 reduce_sum.28
  36.6 0.0 collective-permute-done.1
  36.6 0.2 fusion.11
  36.8 19.9 %collective-permute-done = bf16[256,1024]{1,0:T(8,128)(2,1)S(1)} collective-permute-done((bf16[256,1024]{1,0:T(8,128)(2,1)S(1)}, bf16[256,1024]{1,0:T(8,128)(2,1)S(1)}, u32[]{:S(2)}, u32[]{:S(2)}) %collective-permute-start) | collective-permute-done | bytes 524320 | tf_op jit(solution)/shard_map/ppermute | solution.py:50
  56.7 0.2 fusion.12
  57.0 12.7 %all_to_all.15 = f32[16,8,256]{2,1,0:T(8,128)S(1)} all-to-all(f32[16,8,256]{2,1,0:T(8,128)S(1)} %broadcast_in_dim.37), channel_id=1, replica_groups=mesh['dp'=32,'tensor'=16] {'tensor'}, dimensions={0} | all-to-all | bytes 262144 | tf_op jit(solution)/shard_map/all_to_all | solution.py:71
  69.7 0.6 pad_maximum_fusion.4
  (13 shorter events, 0.2 us)
Async XLA Ops:
  0.0 1.2 %copy-start = (bf16[2,4,256,256]{3,2,1,0:T(8,128)(2,1)S(1)}, bf16[2,4,256,256]{3,2,1,0:T(8,128)(2,1)}, u32[]{:S(2)}) copy-start(bf16[2,4,256,256]{3,2,1,0:T(8,128)(2,1)} %param.7) | copy-start | bytes 3145732
  0.0 15.3 %copy-start.1 = (s32[256]{0:T(256)S(1)}, s32[256]{0:T(256)}, u32[]{:S(2)}) copy-start(s32[256]{0:T(256)} %param.13) | copy-start | bytes 3076
  5.1 20.0 %all-to-all-start = ((bf16[16,128,128]{2,1,0:T(8,128)(2,1)}), bf16[16,128,128]{2,1,0:T(8,128)(2,1)S(1)}, u32[]{:S(2)}, u32[]{:S(2)}) async-start(bf16[16,128,128]{2,1,0:T(8,128)(2,1)} %bitcast.9), calls=%async_computation | async-start | bytes 1048576 | tf_op jit(solution)/shard_map/all_to_all | solution.py:56
  16.6 19.9 %collective-permute-start.1 = (bf16[256,1024]{1,0:T(8,128)(2,1)S(1)}, bf16[256,1024]{1,0:T(8,128)(2,1)S(1)}, u32[]{:S(2)}, u32[]{:S(2)}) collective-permute-start(bf16[256,1024]{1,0:T(8,128)(2,1)S(1)} %convolution_convert_fusion), channel_id=1, source_target_pairs={{0,32},{1,1},{2,34},{3,3},{4,36},{5,5},{6,38},{7,7},{8,40},{9,9},{... | collective-permute-start | bytes 1572872 | tf_op jit(solution)/shard_map/ppermute | solution.py:51
  26.0 10.4 %all-to-all-start.1 = ((f32[16,8,128]{2,1,0:T(8,128)}), f32[16,8,128]{2,1,0:T(8,128)S(1)}, u32[]{:S(2)}, u32[]{:S(2)}) async-start(f32[16,8,128]{2,1,0:T(8,128)} %bitcast.10), calls=%async_computation.1 | async-start | bytes 131072 | tf_op jit(solution)/shard_map/all_to_all | solution.py:61
  30.5 26.1 %collective-permute-start = (bf16[256,1024]{1,0:T(8,128)(2,1)S(1)}, bf16[256,1024]{1,0:T(8,128)(2,1)S(1)}, u32[]{:S(2)}, u32[]{:S(2)}) collective-permute-start(bf16[256,1024]{1,0:T(8,128)(2,1)S(1)} %convolution_convert_fusion), channel_id=1, source_target_pairs={{0,24},{1,57},{2,26},{3,59},{4,28},{5,61},{6,30},{7,63},{8,16},{9,... | collective-permute-start | bytes 1572872 | tf_op jit(solution)/shard_map/ppermute | solution.py:50

commit v9 on v8

--- a/solution.py
+++ b/solution.py
@@ -24,12 +24,10 @@
     return out[: rows.shape[0]] + out[rows.shape[0] :]
 
 
-def project(values, matrix, kept=None):
+def project(values, matrix):
     layers, examples, tokens, width = values.shape
     halves = values.reshape(layers, examples, 2, tokens // 2, width)
     part = jnp.einsum("lehsd,ldr->lehrs", halves, matrix, preferred_element_type=jnp.float32)
-    if kept is not None:
-        part = jnp.where(kept.reshape(1, examples, 2, 1, tokens // 2), part, 0.0)
     return part.astype(jnp.bfloat16)
 
 
@@ -50,21 +48,23 @@
     odd_block = lax.ppermute(ordered, BOTH, block_pairs(shard_count, (1, 3)))
     even_block = lax.ppermute(ordered, BOTH, block_pairs(shard_count, (2, 0)))
 
-    kept = jnp.arange(tokens, dtype=jnp.int32)[None, :] < lengths[:, None]
-    sides = [project(activations, proj_in), project(out_grads, proj_out, kept)]
+    sides = [project(activations, proj_in), project(out_grads, proj_out)]
     part = jnp.concatenate(sides, axis=3).reshape(GROUP, 2 * rank, half_tokens)
     part = lax.all_to_all(part, "tensor", 0, 0)
     proj = jnp.sum(part.astype(jnp.float32), axis=0)
-    outer = jnp.einsum("as,bs->ab", proj[rank:], proj[:rank], precision=HIGH)
+    position = (k & 1) * half_tokens + jnp.arange(half_tokens, dtype=jnp.int32)
+    kept = position < lengths[(k >> 1) & 3]
+    grad = jnp.where(kept[None, :], proj[rank:], 0.0)
+    outer = jnp.einsum("as,bs->ab", grad, proj[:rank], precision=HIGH)
     outer = outer.reshape(1, 4, 1, rank // 8, 2 * rank)
     outer = jnp.broadcast_to(outer, (2, 4, 2, rank // 8, 2 * rank)).reshape(GROUP, rank // 8, 2 * rank)
     outer = lax.all_to_all(outer, "tensor", 0, 0)
     features = outer.reshape(2 * examples, 2, quarter).sum(axis=1)
 
+    swap = layer_one > 0.5
     odd = split_dot(features, odd_block).reshape(2, examples, block)
+    odd = lax.optimization_barrier(jnp.where(swap, odd[0], odd[1]))
     even = split_dot(features, even_block).reshape(2, examples, block)
-    swap = layer_one > 0.5
-    odd = jnp.where(swap, odd[0], odd[1])
     even = jnp.where(swap, even[1], even[0])
     scores = jnp.concatenate([odd, even], axis=0)
     scores = jnp.broadcast_to(scores[None], (GROUP, 2 * examples, block))

time: 70.8 us -> 70.8 us (level)
  local copies, waits for them, and re-layouts: 1.2 us -> 2.61 us
  waiting for transfers between devices: 30.9 us -> 29.6 us
    all_to_all x1, waiting for transfers between devices: 7.68 us -> 6.41 us  [shards(): part = lax.all_to_all(part, 'tensor', 0, 0)]
    unnamed x4 -> x6, local copies, waits for them, and re-layouts: 0.42 us -> 1.23 us
  transfers between devices with their start and end apart: 4 -> 4, of which waited for: 3 -> 3; matrix products, arithmetic and copies ran while one was open for 4% -> 6% of each run, Pallas kernels for 0% -> 0%
where the time goes in v9:
time: 70.8 us; the launch traced here: 70.3 us
  waiting for transfers between devices  29.6 us (42%)
  starting transfers between devices  18 us (25%)
  blocking collectives  12.7 us (18%)
  matrix products  5 us (7%)
  local copies, waits for them, and re-layouts  2.61 us (4%)
  other arithmetic  2.34 us (3%)
    ppermute x1, waiting for transfers between devices, shards(): odd_block = lax.ppermute(ordered, BOTH, block_pairs(shard_count, (1, 3)))  19.9 us
    all_to_all x1, blocking collectives, shards(): scores = lax.all_to_all(scores, 'tensor', 0, 0)  12.7 us
    all_to_all x1, starting transfers between devices, shards(): part = lax.all_to_all(part, 'tensor', 0, 0)  10.2 us
    all_to_all x1, waiting for transfers between devices, shards(): part = lax.all_to_all(part, 'tensor', 0, 0)  6.41 us
    all_to_all x1, starting transfers between devices, shards(): outer = lax.all_to_all(outer, 'tensor', 0, 0)  4.54 us
    all_to_all x1, waiting for transfers between devices, shards(): outer = lax.all_to_all(outer, 'tensor', 0, 0)  3.35 us
    dot_general x2, matrix products, project(): jnp.einsum('lehsd,ldr->lehrs', halves, matrix, preferred_element_type=jnp...  3 us
    ppermute x1, starting transfers between devices, shards(): odd_block = lax.ppermute(ordered, BOTH, block_pairs(shard_count, (1, 3)))  2.54 us
  transfers between devices with their start and end apart: 4, of which 3 were waited for; matrix products, arithmetic and copies ran while one was open for 6% of the time, Pallas kernels for 0%

profile of v9, /device:TPU:1, one launch (start us, length us, event | category | flops | bytes accessed | tf_op | source)
XLA Modules:
  0.0 70.3 jit_solution(14316750232562974179)
XLA Ops:
  0.0 0.0 copy-start
  0.0 0.0 copy-start.1
  0.0 1.2 %copy-done = bf16[2,4,256,256]{3,2,1,0:T(8,128)(2,1)S(1)} copy-done((bf16[2,4,256,256]{3,2,1,0:T(8,128)(2,1)S(1)}, bf16[2,4,256,256]{3,2,1,0:T(8,128)(2,1)}, u32[]{:S(2)}) %copy-start) | copy-done | bytes 1048600
  1.2 0.0 copy-start.2
  1.2 1.3 %fusion = bf16[2,4,2,64,128]{4,3,2,1,0:T(8,128)(2,1)S(1)} fusion(bf16[2,4,2,128,256]{4,3,2,1,0:T(8,128)(2,1)S(1)} %bitcast.34, bf16[2,256,64]{1,2,0:T(8,128)(2,1)} %param.9), kind=kOutput, calls=%fused_computation.3 | convolution fusion | flops 67239936 | bytes 1376256 | tf_op jit(solution)/shard_map/lehsd,ldr->lehrs/dot_general | solution.py:30
  2.5 1.7 %fusion.1 = bf16[2,4,2,64,128]{4,3,2,1,0:T(8,128)(2,1)S(1)} fusion(bf16[2,4,2,128,256]{4,3,2,1,0:T(8,128)(2,1)} %bitcast.35, bf16[2,256,64]{1,2,0:T(8,128)(2,1)} %param.10), kind=kOutput, calls=%fused_computation.4 | convolution fusion | flops 67239936 | bytes 1376256 | tf_op jit(solution)/shard_map/lehsd,ldr->lehrs/dot_general | solution.py:30
  4.2 0.8 %pad_maximum_fusion = bf16[2,4,2,128,128]{4,3,2,1,0:T(8,128)(2,1)} fusion(bf16[2,4,2,64,128]{4,3,2,1,0:T(8,128)(2,1)S(1)} %fusion.1, bf16[2,4,2,64,128]{4,3,2,1,0:T(8,128)(2,1)S(1)} %fusion), kind=kLoop, calls=%fused_computation.6 | loop fusion | flops 1048576 | bytes 1048576 | tf_op jit(solution)/shard_map/concatenate | solution.py:52
  5.1 10.2 %all-to-all-start = ((bf16[16,128,128]{2,1,0:T(8,128)(2,1)}), bf16[16,128,128]{2,1,0:T(8,128)(2,1)S(1)}, u32[]{:S(2)}, u32[]{:S(2)}) async-start(bf16[16,128,128]{2,1,0:T(8,128)(2,1)} %bitcast.10), calls=%async_computation | async-start | bytes 1048576 | tf_op jit(solution)/shard_map/all_to_all | solution.py:53
  15.3 0.0 copy-done.1
  15.3 1.4 %convolution_convert_fusion = bf16[256,1024]{1,0:T(8,128)(2,1)S(1)} fusion(bf16[2,256,4096]{2,1,0:T(8,128)(2,1)} %param.12, s32[]{:T(128)S(6)} %select_n.20, s32[]{:T(128)S(6)} %select_n.21, s32[256]{0:T(256)S(1)} %copy-done.1), kind=kOutput, calls=%fused_computation | convolution fusion | flops 134545408 | bytes 1049608 | tf_op jit(solution)/shard_map/dot_general | solution.py:45
  16.6 0.7 collective-permute-start.1
  17.3 0.0 copy-done.2
  17.4 0.6 dynamic_slice.7
  17.9 0.7 add_compare_fusion
  18.6 6.4 %all-to-all-done = bf16[16,128,128]{2,1,0:T(8,128)(2,1)S(1)} async-done(((bf16[16,128,128]{2,1,0:T(8,128)(2,1)}), bf16[16,128,128]{2,1,0:T(8,128)(2,1)S(1)}, u32[]{:S(2)}, u32[]{:S(2)}) %all-to-all-start) | async-done | bytes 524320 | tf_op jit(solution)/shard_map/all_to_all | solution.py:53
  25.0 0.1 convert_reduce_fusion
  25.1 0.2 fusion.7
  25.3 0.1 broadcast_in_dim.34
  25.4 0.6 broadcast_in_dim.35
  26.0 4.5 %all-to-all-start.1 = ((f32[16,8,128]{2,1,0:T(8,128)}), f32[16,8,128]{2,1,0:T(8,128)S(1)}, u32[]{:S(2)}, u32[]{:S(2)}) async-start(f32[16,8,128]{2,1,0:T(8,128)} %bitcast.11), calls=%async_computation.1 | async-start | bytes 131072 | tf_op jit(solution)/shard_map/all_to_all | solution.py:61
  30.5 2.5 %collective-permute-start = (bf16[256,1024]{1,0:T(8,128)(2,1)S(1)}, bf16[256,1024]{1,0:T(8,128)(2,1)S(1)}, u32[]{:S(2)}, u32[]{:S(2)}) collective-permute-start(bf16[256,1024]{1,0:T(8,128)(2,1)S(1)} %convolution_convert_fusion), channel_id=1, source_target_pairs={{0,24},{1,57},{2,26},{3,59},{4,28},{5,61},{6,30},{7,63},{8,16},{9,... | collective-permute-start | bytes 1572872 | tf_op jit(solution)/shard_map/ppermute | solution.py:48
  33.1 3.3 %all-to-all-done.1 = f32[16,8,128]{2,1,0:T(8,128)S(1)} async-done(((f32[16,8,128]{2,1,0:T(8,128)}), f32[16,8,128]{2,1,0:T(8,128)S(1)}, u32[]{:S(2)}, u32[]{:S(2)}) %all-to-all-start.1) | async-done | bytes 65568 | tf_op jit(solution)/shard_map/all_to_all | solution.py:61
  36.5 0.1 reduce_sum.28
  36.5 0.0 collective-permute-done.1
  36.6 0.2 fusion.9
  36.8 19.9 %collective-permute-done = bf16[256,1024]{1,0:T(8,128)(2,1)S(1)} collective-permute-done((bf16[256,1024]{1,0:T(8,128)(2,1)S(1)}, bf16[256,1024]{1,0:T(8,128)(2,1)S(1)}, u32[]{:S(2)}, u32[]{:S(2)}) %collective-permute-start) | collective-permute-done | bytes 524320 | tf_op jit(solution)/shard_map/ppermute | solution.py:48
  56.7 0.2 fusion.10
  57.0 12.7 %all_to_all.15 = f32[16,8,256]{2,1,0:T(8,128)S(1)} all-to-all(f32[16,8,256]{2,1,0:T(8,128)S(1)} %broadcast_in_dim.36), channel_id=1, replica_groups=mesh['dp'=32,'tensor'=16] {'tensor'}, dimensions={0} | all-to-all | bytes 262144 | tf_op jit(solution)/shard_map/all_to_all | solution.py:71
  69.7 0.6 pad_maximum_fusion.4
  (12 shorter events, 0.2 us)
Async XLA Ops:
  0.0 1.2 %copy-start = (bf16[2,4,256,256]{3,2,1,0:T(8,128)(2,1)S(1)}, bf16[2,4,256,256]{3,2,1,0:T(8,128)(2,1)}, u32[]{:S(2)}) copy-start(bf16[2,4,256,256]{3,2,1,0:T(8,128)(2,1)} %param.7) | copy-start | bytes 3145732
  0.0 15.3 %copy-start.1 = (s32[256]{0:T(256)S(1)}, s32[256]{0:T(256)}, u32[]{:S(2)}) copy-start(s32[256]{0:T(256)} %param.13) | copy-start | bytes 3076
  1.2 16.1 %copy-start.2 = (s32[4]{0:T(128)S(1)}, s32[4]{0:T(128)}, u32[]{:S(2)}) copy-start(s32[4]{0:T(128)} %param.11) | copy-start | bytes 52
  5.1 20.0 %all-to-all-start = ((bf16[16,128,128]{2,1,0:T(8,128)(2,1)}), bf16[16,128,128]{2,1,0:T(8,128)(2,1)S(1)}, u32[]{:S(2)}, u32[]{:S(2)}) async-start(bf16[16,128,128]{2,1,0:T(8,128)(2,1)} %bitcast.10), calls=%async_computation | async-start | bytes 1048576 | tf_op jit(solution)/shard_map/all_to_all | solution.py:53
  16.6 19.9 %collective-permute-start.1 = (bf16[256,1024]{1,0:T(8,128)(2,1)S(1)}, bf16[256,1024]{1,0:T(8,128)(2,1)S(1)}, u32[]{:S(2)}, u32[]{:S(2)}) collective-permute-start(bf16[256,1024]{1,0:T(8,128)(2,1)S(1)} %convolution_convert_fusion), channel_id=1, source_target_pairs={{0,32},{1,1},{2,34},{3,3},{4,36},{5,5},{6,38},{7,7},{8,40},{9,9},{... | collective-permute-start | bytes 1572872 | tf_op jit(solution)/shard_map/ppermute | solution.py:49
  26.0 10.4 %all-to-all-start.1 = ((f32[16,8,128]{2,1,0:T(8,128)}), f32[16,8,128]{2,1,0:T(8,128)S(1)}, u32[]{:S(2)}, u32[]{:S(2)}) async-start(f32[16,8,128]{2,1,0:T(8,128)} %bitcast.11), calls=%async_computation.1 | async-start | bytes 131072 | tf_op jit(solution)/shard_map/all_to_all | solution.py:61
  30.5 26.1 %collective-permute-start = (bf16[256,1024]{1,0:T(8,128)(2,1)S(1)}, bf16[256,1024]{1,0:T(8,128)(2,1)S(1)}, u32[]{:S(2)}, u32[]{:S(2)}) collective-permute-start(bf16[256,1024]{1,0:T(8,128)(2,1)S(1)} %convolution_convert_fusion), channel_id=1, source_target_pairs={{0,24},{1,57},{2,26},{3,59},{4,28},{5,61},{6,30},{7,63},{8,16},{9,... | collective-permute-start | bytes 1572872 | tf_op jit(solution)/shard_map/ppermute | solution.py:48

commit v10 on v9

--- a/solution.py
+++ b/solution.py
@@ -43,7 +43,7 @@
     piece = lax.dynamic_slice(test_feats, start, (1, block, quarter))[0]
     place = (jnp.arange(block, dtype=jnp.int32)[:, None] == test_slot[None, :]).astype(jnp.bfloat16)
     ordered = jnp.dot(place, piece, preferred_element_type=jnp.float32).astype(jnp.bfloat16)
-    layer_one = jnp.broadcast_to((k >> 3).astype(jnp.float32), (examples, block))
+    layer_one = jnp.broadcast_to((k >> 3).astype(jnp.float32), (examples, quarter))
     ordered, layer_one = lax.optimization_barrier((ordered, layer_one))
     odd_block = lax.ppermute(ordered, BOTH, block_pairs(shard_count, (1, 3)))
     even_block = lax.ppermute(ordered, BOTH, block_pairs(shard_count, (2, 0)))
@@ -62,12 +62,11 @@
     features = outer.reshape(2 * examples, 2, quarter).sum(axis=1)
 
     swap = layer_one > 0.5
-    odd = split_dot(features, odd_block).reshape(2, examples, block)
-    odd = lax.optimization_barrier(jnp.where(swap, odd[0], odd[1]))
-    even = split_dot(features, even_block).reshape(2, examples, block)
-    even = jnp.where(swap, even[1], even[0])
-    scores = jnp.concatenate([odd, even], axis=0)
-    scores = jnp.broadcast_to(scores[None], (GROUP, 2 * examples, block))
+    odd_rows = jnp.where(swap, features[:examples], features[examples:])
+    even_rows = jnp.where(swap, features[examples:], features[:examples])
+    odd = lax.optimization_barrier(split_dot(odd_rows, odd_block))
+    even = split_dot(even_rows, even_block)
+    scores = jnp.broadcast_to(jnp.stack([odd, even])[None], (GROUP, 2, examples, block))
     scores = lax.all_to_all(scores, "tensor", 0, 0)
     scores = scores.reshape(GROUP // 2, 2, 2, examples, block).sum(axis=0)
     return jnp.concatenate([scores[1, 1], scores[0, 0], scores[0, 1], scores[1, 0]], axis=1)

time: 70.8 us -> 70.8 us (level)
  no operation moved by 1% of the time
where the time goes in v10:
time: 70.8 us; the launch traced here: 70.3 us
  waiting for transfers between devices  29.6 us (42%)
  starting transfers between devices  18 us (25%)
  blocking collectives  12.7 us (18%)
  matrix products  5 us (7%)
  local copies, waits for them, and re-layouts  2.58 us (4%)
  other arithmetic  2.34 us (3%)
    ppermute x1, waiting for transfers between devices, shards(): odd_block = lax.ppermute(ordered, BOTH, block_pairs(shard_count, (1, 3)))  19.8 us
    all_to_all x1, blocking collectives, shards(): scores = lax.all_to_all(scores, 'tensor', 0, 0)  12.7 us
    all_to_all x1, starting transfers between devices, shards(): part = lax.all_to_all(part, 'tensor', 0, 0)  10.2 us
    all_to_all x1, waiting for transfers between devices, shards(): part = lax.all_to_all(part, 'tensor', 0, 0)  6.41 us
    all_to_all x1, starting transfers between devices, shards(): outer = lax.all_to_all(outer, 'tensor', 0, 0)  4.54 us
    all_to_all x1, waiting for transfers between devices, shards(): outer = lax.all_to_all(outer, 'tensor', 0, 0)  3.35 us
    dot_general x2, matrix products, project(): jnp.einsum('lehsd,ldr->lehrs', halves, matrix, preferred_element_type=jnp...  3 us
    ppermute x1, starting transfers between devices, shards(): odd_block = lax.ppermute(ordered, BOTH, block_pairs(shard_count, (1, 3)))  2.54 us
  transfers between devices with their start and end apart: 4, of which 3 were waited for; matrix products, arithmetic and copies ran while one was open for 6% of the time, Pallas kernels for 0%

profile of v10, /device:TPU:1, one launch (start us, length us, event | category | flops | bytes accessed | tf_op | source)
XLA Modules:
  0.0 70.3 jit_solution(3701880408546153721)
XLA Ops:
  0.0 0.0 copy-start
  0.0 0.0 copy-start.1
  0.0 1.2 %copy-done = bf16[2,4,256,256]{3,2,1,0:T(8,128)(2,1)S(1)} copy-done((bf16[2,4,256,256]{3,2,1,0:T(8,128)(2,1)S(1)}, bf16[2,4,256,256]{3,2,1,0:T(8,128)(2,1)}, u32[]{:S(2)}) %copy-start) | copy-done | bytes 1048600
  1.2 0.0 copy-start.2
  1.2 1.3 %fusion = bf16[2,4,2,64,128]{4,3,2,1,0:T(8,128)(2,1)S(1)} fusion(bf16[2,4,2,128,256]{4,3,2,1,0:T(8,128)(2,1)S(1)} %bitcast.38, bf16[2,256,64]{1,2,0:T(8,128)(2,1)} %param.9), kind=kOutput, calls=%fused_computation.3 | convolution fusion | flops 67239936 | bytes 1376256 | tf_op jit(solution)/shard_map/lehsd,ldr->lehrs/dot_general | solution.py:30
  2.5 1.7 %fusion.1 = bf16[2,4,2,64,128]{4,3,2,1,0:T(8,128)(2,1)S(1)} fusion(bf16[2,4,2,128,256]{4,3,2,1,0:T(8,128)(2,1)} %bitcast.39, bf16[2,256,64]{1,2,0:T(8,128)(2,1)} %param.10), kind=kOutput, calls=%fused_computation.4 | convolution fusion | flops 67239936 | bytes 1376256 | tf_op jit(solution)/shard_map/lehsd,ldr->lehrs/dot_general | solution.py:30
  4.2 0.8 %pad_maximum_fusion = bf16[2,4,2,128,128]{4,3,2,1,0:T(8,128)(2,1)} fusion(bf16[2,4,2,64,128]{4,3,2,1,0:T(8,128)(2,1)S(1)} %fusion.1, bf16[2,4,2,64,128]{4,3,2,1,0:T(8,128)(2,1)S(1)} %fusion), kind=kLoop, calls=%fused_computation.6 | loop fusion | flops 1048576 | bytes 1048576 | tf_op jit(solution)/shard_map/concatenate | solution.py:52
  5.1 10.2 %all-to-all-start = ((bf16[16,128,128]{2,1,0:T(8,128)(2,1)}), bf16[16,128,128]{2,1,0:T(8,128)(2,1)S(1)}, u32[]{:S(2)}, u32[]{:S(2)}) async-start(bf16[16,128,128]{2,1,0:T(8,128)(2,1)} %bitcast.10), calls=%async_computation | async-start | bytes 1048576 | tf_op jit(solution)/shard_map/all_to_all | solution.py:53
  15.3 0.0 copy-done.1
  15.3 1.4 %convolution_convert_fusion = bf16[256,1024]{1,0:T(8,128)(2,1)S(1)} fusion(bf16[2,256,4096]{2,1,0:T(8,128)(2,1)} %param.12, s32[]{:T(128)S(6)} %select_n.20, s32[]{:T(128)S(6)} %select_n.21, s32[256]{0:T(256)S(1)} %copy-done.1), kind=kOutput, calls=%fused_computation | convolution fusion | flops 134545408 | bytes 1049608 | tf_op jit(solution)/shard_map/dot_general | solution.py:45
  16.6 0.7 collective-permute-start.1
  17.3 0.0 copy-done.2
  17.4 0.6 dynamic_slice.7
  17.9 0.7 add_compare_fusion
  18.6 6.4 %all-to-all-done = bf16[16,128,128]{2,1,0:T(8,128)(2,1)S(1)} async-done(((bf16[16,128,128]{2,1,0:T(8,128)(2,1)}), bf16[16,128,128]{2,1,0:T(8,128)(2,1)S(1)}, u32[]{:S(2)}, u32[]{:S(2)}) %all-to-all-start) | async-done | bytes 524320 | tf_op jit(solution)/shard_map/all_to_all | solution.py:53
  25.0 0.1 convert_reduce_fusion
  25.1 0.2 fusion.7
  25.3 0.1 broadcast_in_dim.34
  25.4 0.6 broadcast_in_dim.35
  26.0 4.5 %all-to-all-start.1 = ((f32[16,8,128]{2,1,0:T(8,128)}), f32[16,8,128]{2,1,0:T(8,128)S(1)}, u32[]{:S(2)}, u32[]{:S(2)}) async-start(f32[16,8,128]{2,1,0:T(8,128)} %bitcast.11), calls=%async_computation.1 | async-start | bytes 131072 | tf_op jit(solution)/shard_map/all_to_all | solution.py:61
  30.5 2.5 %collective-permute-start = (bf16[256,1024]{1,0:T(8,128)(2,1)S(1)}, bf16[256,1024]{1,0:T(8,128)(2,1)S(1)}, u32[]{:S(2)}, u32[]{:S(2)}) collective-permute-start(bf16[256,1024]{1,0:T(8,128)(2,1)S(1)} %convolution_convert_fusion), channel_id=1, source_target_pairs={{0,24},{1,57},{2,26},{3,59},{4,28},{5,61},{6,30},{7,63},{8,16},{9,... | collective-permute-start | bytes 1572872 | tf_op jit(solution)/shard_map/ppermute | solution.py:48
  33.1 3.3 %all-to-all-done.1 = f32[16,8,128]{2,1,0:T(8,128)S(1)} async-done(((f32[16,8,128]{2,1,0:T(8,128)}), f32[16,8,128]{2,1,0:T(8,128)S(1)}, u32[]{:S(2)}, u32[]{:S(2)}) %all-to-all-start.1) | async-done | bytes 65568 | tf_op jit(solution)/shard_map/all_to_all | solution.py:61
  36.5 0.1 reduce_sum.28
  36.6 0.0 collective-permute-done.1
  36.6 0.2 fusion.13
  36.8 19.8 %collective-permute-done = bf16[256,1024]{1,0:T(8,128)(2,1)S(1)} collective-permute-done((bf16[256,1024]{1,0:T(8,128)(2,1)S(1)}, bf16[256,1024]{1,0:T(8,128)(2,1)S(1)}, u32[]{:S(2)}, u32[]{:S(2)}) %collective-permute-start) | collective-permute-done | bytes 524320 | tf_op jit(solution)/shard_map/ppermute | solution.py:48
  56.7 0.2 fusion.9
  57.0 12.7 %all_to_all.15 = f32[16,2,4,256]{3,2,1,0:T(4,128)S(1)} all-to-all(f32[16,2,4,256]{3,2,1,0:T(4,128)S(1)} %broadcast_in_dim.36), channel_id=1, replica_groups=mesh['dp'=32,'tensor'=16] {'tensor'}, dimensions={0} | all-to-all | bytes 262144 | tf_op jit(solution)/shard_map/all_to_all | solution.py:70
  69.6 0.6 pad_maximum_fusion.1
  (10 shorter events, 0.2 us)
Async XLA Ops:
  0.0 1.2 %copy-start = (bf16[2,4,256,256]{3,2,1,0:T(8,128)(2,1)S(1)}, bf16[2,4,256,256]{3,2,1,0:T(8,128)(2,1)}, u32[]{:S(2)}) copy-start(bf16[2,4,256,256]{3,2,1,0:T(8,128)(2,1)} %param.7) | copy-start | bytes 3145732
  0.0 15.3 %copy-start.1 = (s32[256]{0:T(256)S(1)}, s32[256]{0:T(256)}, u32[]{:S(2)}) copy-start(s32[256]{0:T(256)} %param.13) | copy-start | bytes 3076
  1.2 16.1 %copy-start.2 = (s32[4]{0:T(128)S(1)}, s32[4]{0:T(128)}, u32[]{:S(2)}) copy-start(s32[4]{0:T(128)} %param.11) | copy-start | bytes 52
  5.1 20.0 %all-to-all-start = ((bf16[16,128,128]{2,1,0:T(8,128)(2,1)}), bf16[16,128,128]{2,1,0:T(8,128)(2,1)S(1)}, u32[]{:S(2)}, u32[]{:S(2)}) async-start(bf16[16,128,128]{2,1,0:T(8,128)(2,1)} %bitcast.10), calls=%async_computation | async-start | bytes 1048576 | tf_op jit(solution)/shard_map/all_to_all | solution.py:53
  16.6 19.9 %collective-permute-start.1 = (bf16[256,1024]{1,0:T(8,128)(2,1)S(1)}, bf16[256,1024]{1,0:T(8,128)(2,1)S(1)}, u32[]{:S(2)}, u32[]{:S(2)}) collective-permute-start(bf16[256,1024]{1,0:T(8,128)(2,1)S(1)} %convolution_convert_fusion), channel_id=1, source_target_pairs={{0,32},{1,1},{2,34},{3,3},{4,36},{5,5},{6,38},{7,7},{8,40},{9,9},{... | collective-permute-start | bytes 1572872 | tf_op jit(solution)/shard_map/ppermute | solution.py:49
  26.0 10.4 %all-to-all-start.1 = ((f32[16,8,128]{2,1,0:T(8,128)}), f32[16,8,128]{2,1,0:T(8,128)S(1)}, u32[]{:S(2)}, u32[]{:S(2)}) async-start(f32[16,8,128]{2,1,0:T(8,128)} %bitcast.11), calls=%async_computation.1 | async-start | bytes 131072 | tf_op jit(solution)/shard_map/all_to_all | solution.py:61
  30.5 26.1 %collective-permute-start = (bf16[256,1024]{1,0:T(8,128)(2,1)S(1)}, bf16[256,1024]{1,0:T(8,128)(2,1)S(1)}, u32[]{:S(2)}, u32[]{:S(2)}) collective-permute-start(bf16[256,1024]{1,0:T(8,128)(2,1)S(1)} %convolution_convert_fusion), channel_id=1, source_target_pairs={{0,24},{1,57},{2,26},{3,59},{4,28},{5,61},{6,30},{7,63},{8,16},{9,... | collective-permute-start | bytes 1572872 | tf_op jit(solution)/shard_map/ppermute | solution.py:48

commit v11 on v10

--- a/solution.py
+++ b/solution.py
@@ -43,8 +43,6 @@
     piece = lax.dynamic_slice(test_feats, start, (1, block, quarter))[0]
     place = (jnp.arange(block, dtype=jnp.int32)[:, None] == test_slot[None, :]).astype(jnp.bfloat16)
     ordered = jnp.dot(place, piece, preferred_element_type=jnp.float32).astype(jnp.bfloat16)
-    layer_one = jnp.broadcast_to((k >> 3).astype(jnp.float32), (examples, quarter))
-    ordered, layer_one = lax.optimization_barrier((ordered, layer_one))
     odd_block = lax.ppermute(ordered, BOTH, block_pairs(shard_count, (1, 3)))
     even_block = lax.ppermute(ordered, BOTH, block_pairs(shard_count, (2, 0)))
 
@@ -52,6 +50,8 @@
     part = jnp.concatenate(sides, axis=3).reshape(GROUP, 2 * rank, half_tokens)
     part = lax.all_to_all(part, "tensor", 0, 0)
     proj = jnp.sum(part.astype(jnp.float32), axis=0)
+    layer_one = jnp.broadcast_to((k >> 3).astype(jnp.float32), (examples, quarter))
+    proj, layer_one = lax.optimization_barrier((proj, layer_one))
     position = (k & 1) * half_tokens + jnp.arange(half_tokens, dtype=jnp.int32)
     kept = position < lengths[(k >> 1) & 3]
     grad = jnp.where(kept[None, :], proj[rank:], 0.0)
@@ -66,7 +66,8 @@
     even_rows = jnp.where(swap, features[examples:], features[:examples])
     odd = lax.optimization_barrier(split_dot(odd_rows, odd_block))
     even = split_dot(even_rows, even_block)
-    scores = jnp.broadcast_to(jnp.stack([odd, even])[None], (GROUP, 2, examples, block))
+    scores = jnp.concatenate([odd, even], axis=0)
+    scores = jnp.broadcast_to(scores[None], (GROUP, 2 * examples, block))
     scores = lax.all_to_all(scores, "tensor", 0, 0)
     scores = scores.reshape(GROUP // 2, 2, 2, examples, block).sum(axis=0)
     return jnp.concatenate([scores[1, 1], scores[0, 0], scores[0, 1], scores[1, 0]], axis=1)

time: 70.8 us -> 70.8 us (level)
  no operation moved by 1% of the time
where the time goes in v11:
time: 70.8 us; the launch traced here: 70.3 us
  waiting for transfers between devices  29.6 us (42%)
  starting transfers between devices  18 us (25%)
  blocking collectives  12.7 us (18%)
  matrix products  5 us (7%)
  local copies, waits for them, and re-layouts  2.61 us (4%)
  other arithmetic  2.35 us (3%)
    ppermute x1, waiting for transfers between devices, shards(): odd_block = lax.ppermute(ordered, BOTH, block_pairs(shard_count, (1, 3)))  19.8 us
    all_to_all x1, blocking collectives, shards(): scores = lax.all_to_all(scores, 'tensor', 0, 0)  12.7 us
    all_to_all x1, starting transfers between devices, shards(): part = lax.all_to_all(part, 'tensor', 0, 0)  10.2 us
    all_to_all x1, waiting for transfers between devices, shards(): part = lax.all_to_all(part, 'tensor', 0, 0)  6.42 us
    all_to_all x1, starting transfers between devices, shards(): outer = lax.all_to_all(outer, 'tensor', 0, 0)  4.54 us
    all_to_all x1, waiting for transfers between devices, shards(): outer = lax.all_to_all(outer, 'tensor', 0, 0)  3.35 us
    dot_general x2, matrix products, project(): jnp.einsum('lehsd,ldr->lehrs', halves, matrix, preferred_element_type=jnp...  3 us
    ppermute x1, starting transfers between devices, shards(): odd_block = lax.ppermute(ordered, BOTH, block_pairs(shard_count, (1, 3)))  2.54 us
  transfers between devices with their start and end apart: 4, of which 3 were waited for; matrix products, arithmetic and copies ran while one was open for 6% of the time, Pallas kernels for 0%

profile of v11, /device:TPU:1, one launch (start us, length us, event | category | flops | bytes accessed | tf_op | source)
XLA Modules:
  0.0 70.3 jit_solution(9405312930255142048)
XLA Ops:
  0.0 0.0 copy-start
  0.0 0.0 copy-start.1
  0.0 1.2 %copy-done = bf16[2,4,256,256]{3,2,1,0:T(8,128)(2,1)S(1)} copy-done((bf16[2,4,256,256]{3,2,1,0:T(8,128)(2,1)S(1)}, bf16[2,4,256,256]{3,2,1,0:T(8,128)(2,1)}, u32[]{:S(2)}) %copy-start) | copy-done | bytes 1048600
  1.2 0.0 copy-start.2
  1.2 1.3 %fusion = bf16[2,4,2,64,128]{4,3,2,1,0:T(8,128)(2,1)S(1)} fusion(bf16[2,4,2,128,256]{4,3,2,1,0:T(8,128)(2,1)S(1)} %bitcast.34, bf16[2,256,64]{1,2,0:T(8,128)(2,1)} %param.9), kind=kOutput, calls=%fused_computation.3 | convolution fusion | flops 67239936 | bytes 1376256 | tf_op jit(solution)/shard_map/lehsd,ldr->lehrs/dot_general | solution.py:30
  2.5 1.7 %fusion.1 = bf16[2,4,2,64,128]{4,3,2,1,0:T(8,128)(2,1)S(1)} fusion(bf16[2,4,2,128,256]{4,3,2,1,0:T(8,128)(2,1)} %bitcast.35, bf16[2,256,64]{1,2,0:T(8,128)(2,1)} %param.10), kind=kOutput, calls=%fused_computation.4 | convolution fusion | flops 67239936 | bytes 1376256 | tf_op jit(solution)/shard_map/lehsd,ldr->lehrs/dot_general | solution.py:30
  4.2 0.8 %pad_maximum_fusion = bf16[2,4,2,128,128]{4,3,2,1,0:T(8,128)(2,1)} fusion(bf16[2,4,2,64,128]{4,3,2,1,0:T(8,128)(2,1)S(1)} %fusion.1, bf16[2,4,2,64,128]{4,3,2,1,0:T(8,128)(2,1)S(1)} %fusion), kind=kLoop, calls=%fused_computation.6 | loop fusion | flops 1048576 | bytes 1048576 | tf_op jit(solution)/shard_map/concatenate | solution.py:50
  5.1 10.2 %all-to-all-start = ((bf16[16,128,128]{2,1,0:T(8,128)(2,1)}), bf16[16,128,128]{2,1,0:T(8,128)(2,1)S(1)}, u32[]{:S(2)}, u32[]{:S(2)}) async-start(bf16[16,128,128]{2,1,0:T(8,128)(2,1)} %bitcast.8), calls=%async_computation | async-start | bytes 1048576 | tf_op jit(solution)/shard_map/all_to_all | solution.py:51
  15.3 0.0 copy-done.1
  15.3 1.4 %convolution_convert_fusion = bf16[256,1024]{1,0:T(8,128)(2,1)S(1)} fusion(bf16[2,256,4096]{2,1,0:T(8,128)(2,1)} %param.12, s32[]{:T(128)S(6)} %select_n.23, s32[]{:T(128)S(6)} %select_n.24, s32[256]{0:T(256)S(1)} %copy-done.1), kind=kOutput, calls=%fused_computation | convolution fusion | flops 134545408 | bytes 1049608 | tf_op jit(solution)/shard_map/dot_general | solution.py:45
  16.6 0.7 collective-permute-start.1
  17.3 0.0 copy-done.2
  17.3 0.6 dynamic_slice.6
  17.9 0.7 add_compare_fusion
  18.6 6.4 %all-to-all-done = bf16[16,128,128]{2,1,0:T(8,128)(2,1)S(1)} async-done(((bf16[16,128,128]{2,1,0:T(8,128)(2,1)}), bf16[16,128,128]{2,1,0:T(8,128)(2,1)S(1)}, u32[]{:S(2)}, u32[]{:S(2)}) %all-to-all-start) | async-done | bytes 524320 | tf_op jit(solution)/shard_map/all_to_all | solution.py:51
  25.0 0.1 convert_reduce_fusion
  25.1 0.2 fusion.7
  25.3 0.1 broadcast_in_dim.34
  25.4 0.6 broadcast_in_dim.35
  26.0 4.5 %all-to-all-start.1 = ((f32[16,8,128]{2,1,0:T(8,128)}), f32[16,8,128]{2,1,0:T(8,128)S(1)}, u32[]{:S(2)}, u32[]{:S(2)}) async-start(f32[16,8,128]{2,1,0:T(8,128)} %bitcast.10), calls=%async_computation.1 | async-start | bytes 131072 | tf_op jit(solution)/shard_map/all_to_all | solution.py:61
  30.5 2.5 %collective-permute-start = (bf16[256,1024]{1,0:T(8,128)(2,1)S(1)}, bf16[256,1024]{1,0:T(8,128)(2,1)S(1)}, u32[]{:S(2)}, u32[]{:S(2)}) collective-permute-start(bf16[256,1024]{1,0:T(8,128)(2,1)S(1)} %convolution_convert_fusion), channel_id=1, source_target_pairs={{0,24},{1,57},{2,26},{3,59},{4,28},{5,61},{6,30},{7,63},{8,16},{9,... | collective-permute-start | bytes 1572872 | tf_op jit(solution)/shard_map/ppermute | solution.py:46
  33.1 3.3 %all-to-all-done.1 = f32[16,8,128]{2,1,0:T(8,128)S(1)} async-done(((f32[16,8,128]{2,1,0:T(8,128)}), f32[16,8,128]{2,1,0:T(8,128)S(1)}, u32[]{:S(2)}, u32[]{:S(2)}) %all-to-all-start.1) | async-done | bytes 65568 | tf_op jit(solution)/shard_map/all_to_all | solution.py:61
  36.5 0.1 reduce_sum.28
  36.6 0.0 collective-permute-done.1
  36.6 0.2 fusion.15
  36.8 19.8 %collective-permute-done = bf16[256,1024]{1,0:T(8,128)(2,1)S(1)} collective-permute-done((bf16[256,1024]{1,0:T(8,128)(2,1)S(1)}, bf16[256,1024]{1,0:T(8,128)(2,1)S(1)}, u32[]{:S(2)}, u32[]{:S(2)}) %collective-permute-start) | collective-permute-done | bytes 524320 | tf_op jit(solution)/shard_map/ppermute | solution.py:46
  56.7 0.2 fusion.11
  57.0 12.7 %all_to_all.15 = f32[16,8,256]{2,1,0:T(8,128)S(1)} all-to-all(f32[16,8,256]{2,1,0:T(8,128)S(1)} %broadcast_in_dim.36), channel_id=1, replica_groups=mesh['dp'=32,'tensor'=16] {'tensor'}, dimensions={0} | all-to-all | bytes 262144 | tf_op jit(solution)/shard_map/all_to_all | solution.py:71
  69.7 0.6 pad_maximum_fusion.1
  (11 shorter events, 0.2 us)
Async XLA Ops:
  0.0 1.2 %copy-start = (bf16[2,4,256,256]{3,2,1,0:T(8,128)(2,1)S(1)}, bf16[2,4,256,256]{3,2,1,0:T(8,128)(2,1)}, u32[]{:S(2)}) copy-start(bf16[2,4,256,256]{3,2,1,0:T(8,128)(2,1)} %param.7) | copy-start | bytes 3145732
  0.0 15.3 %copy-start.1 = (s32[256]{0:T(256)S(1)}, s32[256]{0:T(256)}, u32[]{:S(2)}) copy-start(s32[256]{0:T(256)} %param.13) | copy-start | bytes 3076
  1.2 16.1 %copy-start.2 = (s32[4]{0:T(128)S(1)}, s32[4]{0:T(128)}, u32[]{:S(2)}) copy-start(s32[4]{0:T(128)} %param.11) | copy-start | bytes 52
  5.1 20.0 %all-to-all-start = ((bf16[16,128,128]{2,1,0:T(8,128)(2,1)}), bf16[16,128,128]{2,1,0:T(8,128)(2,1)S(1)}, u32[]{:S(2)}, u32[]{:S(2)}) async-start(bf16[16,128,128]{2,1,0:T(8,128)(2,1)} %bitcast.8), calls=%async_computation | async-start | bytes 1048576 | tf_op jit(solution)/shard_map/all_to_all | solution.py:51
  16.6 20.0 %collective-permute-start.1 = (bf16[256,1024]{1,0:T(8,128)(2,1)S(1)}, bf16[256,1024]{1,0:T(8,128)(2,1)S(1)}, u32[]{:S(2)}, u32[]{:S(2)}) collective-permute-start(bf16[256,1024]{1,0:T(8,128)(2,1)S(1)} %convolution_convert_fusion), channel_id=1, source_target_pairs={{0,32},{1,1},{2,34},{3,3},{4,36},{5,5},{6,38},{7,7},{8,40},{9,9},{... | collective-permute-start | bytes 1572872 | tf_op jit(solution)/shard_map/ppermute | solution.py:47
  26.0 10.4 %all-to-all-start.1 = ((f32[16,8,128]{2,1,0:T(8,128)}), f32[16,8,128]{2,1,0:T(8,128)S(1)}, u32[]{:S(2)}, u32[]{:S(2)}) async-start(f32[16,8,128]{2,1,0:T(8,128)} %bitcast.10), calls=%async_computation.1 | async-start | bytes 131072 | tf_op jit(solution)/shard_map/all_to_all | solution.py:61
  30.5 26.1 %collective-permute-start = (bf16[256,1024]{1,0:T(8,128)(2,1)S(1)}, bf16[256,1024]{1,0:T(8,128)(2,1)S(1)}, u32[]{:S(2)}, u32[]{:S(2)}) collective-permute-start(bf16[256,1024]{1,0:T(8,128)(2,1)S(1)} %convolution_convert_fusion), channel_id=1, source_target_pairs={{0,24},{1,57},{2,26},{3,59},{4,28},{5,61},{6,30},{7,63},{8,16},{9,... | collective-permute-start | bytes 1572872 | tf_op jit(solution)/shard_map/ppermute | solution.py:46
